TPU v7x, 32 devices: a whole 2x2x4 slice. The times are simulated.
32 devices in a mesh: grp: 4 (over x, core), pen: 8 (over z, y).
Axes of the slice: x: 2, y: 2, z: 4, core: 2. Of those that a mesh axis runs over, the one named last changes fastest.
Arguments:
- u_field: float32 [2, 2048, 2048], P(None, ('grp', 'pen')), may hold values from -6 to 6
- v_field: float32 [2, 2048, 2048], P(None, ('grp', 'pen')), may hold values from -6 to 6
- ky_order: int32 [2048], replicated, may hold values from 0 to 2047, as said below
Outputs:
- deriv: float32 [2048, 2, 2, 2048], P('grp', None, None, 'pen')
Inputs may be any that keep to these rules, and one draw needn't show every extreme that they name: ky_order is a permutation of 0 to 2047; for every position j, ky_order[2047 - j] = (2048 - ky_order[j]) mod 2048, except for the one pair of positions that holds 0 and 1024.
All inputs are finite; a program needn't handle non-finite values.
Results may differ from a plain program's by a relative error of at most 0.00007.
Values sent between devices are 32-bit elements; how exact they have to be, the bound alone decides.
No kernel may reach another device: no remote copies, remote signals or barrier semaphores. Data moves between devices by JAX's collectives and lax.ppermute only.
A program may use at most 64 MiB of HBM per device.

v0:
```python
import math

import jax
import jax.numpy as jnp
from jax import lax
from jax.sharding import PartitionSpec as P

two_pi = 2.0 * math.pi


def partner_2(block, axis, bit):
    count = lax.axis_size(axis)
    route = []
    for low in range(count):
        high = low | 1 << bit
        if high != low and high < count:
            route += [(low, high), (high, low)]
    return lax.ppermute(block, axis, route)


def signed_scale(waves, length):
    signed = jnp.where(waves < length // 2, waves, waves - length)
    signed = jnp.where(waves == length // 2, 0, signed)
    return 2.0 / length * signed.astype(jnp.float32)


def twiddle(row_values, column_values, length):
    residue = row_values[:, None] * column_values[None, :] % length
    angles = two_pi / length * residue.astype(jnp.float32)
    return (jnp.cos(angles), jnp.sin(angles))


def wave_numbers(position, length, group_rows):
    half_length = length // 2
    quarter = position // group_rows
    local_row = position - quarter * group_rows
    mirrored = group_rows - 1 - local_row
    upper_side = local_row >= group_rows // 2
    pair_index = quarter * (group_rows // 2) + jnp.minimum(local_row, mirrored)
    upper_value = jnp.where(pair_index > 0, length - pair_index, half_length)
    return (jnp.where(upper_side, upper_value, pair_index), pair_index == 0)


def on_device(u_field, v_field, ky_order):
    planes, entry_rows, length_y = u_field.shape
    pen_size = lax.axis_size("pen")
    group_size = lax.axis_size("grp")
    quarter = lax.axis_index("grp")
    slab_rows = length_y // pen_size
    group_rows = entry_rows * pen_size
    length_z = group_rows * group_size
    column_count = planes * slab_rows
    exact_mode = lax.Precision.HIGHEST
    stacked = jnp.concatenate([u_field, v_field], 0).reshape(2 * planes * entry_rows, length_y)
    positions_y = lax.iota(jnp.int32, length_y)
    block_width = min(length_y, 128)
    block_count = length_y // block_width

    def row_block(first_row):
        waves_y = lax.dynamic_slice_in_dim(ky_order, first_row, block_width)
        cosines, sines = twiddle(positions_y, waves_y, length_y)
        tables = jnp.concatenate([cosines, sines], 1)
        return jnp.dot(stacked, tables, precision=exact_mode, preferred_element_type=jnp.float32)

    blocks = lax.map(row_block, jnp.arange(block_count, dtype=jnp.int32) * block_width)
    pieces = blocks.reshape(block_count, 2, planes * entry_rows, 2, block_width)
    norm_y = 1.0 / math.sqrt(length_y)

    def to_layout(values):
        return (norm_y * jnp.transpose(values, (1, 0, 2))).reshape(planes, entry_rows, length_y)

    real_rows = to_layout(pieces[:, 0, :, 0] + pieces[:, 1, :, 1])
    imaginary_rows = to_layout(pieces[:, 1, :, 0] - pieces[:, 0, :, 1])

    def as_columns(values):
        return jnp.transpose(values, (1, 0, 2)).reshape(group_rows, column_count)

    my_waves_y = lax.dynamic_slice_in_dim(ky_order, lax.axis_index("pen") * slab_rows, slab_rows)
    self_y = (my_waves_y == 0) | (my_waves_y == length_y // 2)
    own_z = quarter * group_rows + lax.iota(jnp.int32, group_rows)
    own_waves_z, self_z = wave_numbers(own_z, length_z, group_rows)
    norm_z = 1.0 / math.sqrt(length_z)
    received = (
        lax.all_to_all(real_rows, "pen", split_axis=2, concat_axis=1, tiled=True),
        lax.all_to_all(imaginary_rows, "pen", split_axis=2, concat_axis=1, tiled=True),
    )
    right_side = jnp.concatenate([as_columns(values) for values in received], 1)
    pair_count = len(received) // 2
    block_rows = math.gcd(group_rows * lax.axis_size("grp"), 256)

    def forward_block_term(offset):
        position = offset + lax.iota(jnp.int32, block_rows)
        waves_z, unused = wave_numbers(position, length_z, group_rows)
        cosines, sines = twiddle(waves_z, own_z, length_z)
        left_side = jnp.concatenate([cosines, sines], 0)
        product = jnp.dot(
            left_side, right_side, precision=exact_mode, preferred_element_type=jnp.float32
        )
        product = product.reshape(2, block_rows, pair_count, 2, column_count)
        real_part = product[0, :, :, 0] + product[1, :, :, 1]
        imaginary_part = product[0, :, :, 1] - product[1, :, :, 0]
        return norm_z * jnp.stack([real_part, imaginary_part], 2).reshape(block_rows, -1)

    offsets = (
        jnp.arange(group_rows * lax.axis_size("grp") // block_rows, dtype=jnp.int32) * block_rows
    )
    spectrum = lax.psum_scatter(
        lax.map(forward_block_term, offsets).reshape(group_rows * lax.axis_size("grp"), -1),
        "grp",
        scatter_dimension=0,
        tiled=True,
    )
    own_part = spectrum.reshape(group_rows, 2, planes, slab_rows)
    partner = spectrum
    for level in range(pen_size.bit_length() - 1):
        partner = partner_2(partner, "pen", level)
    partner = jnp.flip(partner.reshape(group_rows, 2, planes, slab_rows), 3)
    chosen = jnp.where(self_y[None, None, None, :], own_part, partner)
    across = chosen
    across = jnp.flip(across, 0)
    mirror = jnp.where(self_z[:, None, None, None], chosen, across)
    own_real, own_imag = (own_part[:, 0], own_part[:, 1])
    mirror_real, mirror_imag = (mirror[:, 0], mirror[:, 1])
    first_real = 0.5 * (own_real + mirror_real)
    first_imag = 0.5 * (own_imag - mirror_imag)
    second_real = 0.5 * (own_imag + mirror_imag)
    second_imag = -0.5 * (own_real - mirror_real)
    scale_y = signed_scale(my_waves_y, length_y)[None, None, :]
    scale_z = signed_scale(own_waves_z, length_z)[:, None, None]
    packed_real = -scale_y * first_imag - scale_z * second_real
    packed_imag = scale_y * first_real - scale_z * second_imag
    back_side = jnp.concatenate(
        [
            packed_real.reshape(group_rows, column_count),
            packed_imag.reshape(group_rows, column_count),
        ],
        1,
    )
    inverse_block_rows = math.gcd(group_rows * lax.axis_size("grp"), 256)

    def inverse_block_term(offset):
        position = offset + lax.iota(jnp.int32, inverse_block_rows)
        cosines, sines = twiddle(position, own_waves_z, length_z)
        left_side = jnp.concatenate([cosines, sines], 0)
        product = jnp.dot(
            left_side, back_side, precision=exact_mode, preferred_element_type=jnp.float32
        )
        product = product.reshape(2, inverse_block_rows, 2, column_count)
        real_part = product[0, :, 0] - product[1, :, 1]
        imaginary_part = product[0, :, 1] + product[1, :, 0]
        return norm_z * jnp.stack([real_part, imaginary_part], 1).reshape(inverse_block_rows, -1)

    offsets = (
        jnp.arange(group_rows * lax.axis_size("grp") // inverse_block_rows, dtype=jnp.int32)
        * inverse_block_rows
    )
    result = lax.psum_scatter(
        lax.map(inverse_block_term, offsets).reshape(group_rows * lax.axis_size("grp"), -1),
        "grp",
        scatter_dimension=0,
        tiled=True,
    )
    return result.reshape(group_rows, 2, planes, slab_rows)


def solution(mesh):
    placed = (P(None, ("grp", "pen"), None), P(None, ("grp", "pen"), None), P())
    return jax.shard_map(
        on_device,
        mesh=mesh,
        in_specs=placed,
        out_specs=P("grp", None, None, "pen"),
        check_vma=False,
    )
```

profile of v0, /device:TPU:0, one launch (start us, length us, event | category | flops | bytes accessed | tf_op | source)
XLA Modules:
  0.0 977.8 jit_solution(1435095933212386418)
XLA Ops:
  8.2 191.2 %while.39 = (s32[]{:T(128)}, f32[16,256,256]{1,2,0:T(8,128)}, s32[16]{0:T(128)S(1)}, s32[2048]{0:T(1024)}, f32[256,2048]{1,0:T(8,128)S(1)}, /*index=5*/s32[]{:T(128)}, s32[]{:T(128)}, s32[]{:T(128)}) while((s32[]{:T(128)}, f32[16,256,256]{1,2,0:T(8,128)}, s32[16]{0:T(128)S(1)}, s32[2048]{0:T(1024)}, f32[256,2048]{1,0:T(8,128)S(1)}, ...), condition=%wide.region_1.2_spmd.clone, body=%wide.region_0.1_spmd.clone.sunk | while | flops 1614807040 | bytes 6555783 | solution.py:65
  11.8 4.1 fusion.86
  15.9 4.3 fusion.87
  23.7 4.1 fusion.86
  27.8 4.3 fusion.87
  35.6 4.1 fusion.86
  39.7 4.3 fusion.87
  47.6 4.1 fusion.86
  51.7 4.3 fusion.87
  59.5 4.1 fusion.86
  63.6 4.4 fusion.87
  71.5 4.1 fusion.86
  75.6 4.3 fusion.87
  83.4 4.1 fusion.86
  87.5 4.3 fusion.87
  95.4 4.1 fusion.86
  99.5 4.4 fusion.87
  107.4 4.1 fusion.86
  111.5 4.3 fusion.87
  119.3 4.1 fusion.86
  123.4 4.3 fusion.87
  135.4 4.4 fusion.87
  143.2 4.1 fusion.86
  147.3 4.3 fusion.87
  159.3 4.3 fusion.87
  171.2 4.3 fusion.87
  183.1 4.3 fusion.87
  195.1 4.3 fusion.87
  199.4 5.8 reshape.307
  205.2 8.0 fusion.65
  221.7 7.4 all-to-all-start
  237.3 17.7 %all-to-all-done = f32[8,1,32768]{2,1,0:T(1,128)} async-done(((f32[8,1,32768]{2,1,0:T(1,128)}), f32[8,1,32768]{2,1,0:T(1,128)}, u32[]{:S(2)}, u32[]{:S(2)}) %all-to-all-start) | async-done | bytes 1048608 | tf_op jit(solution)/shard_map/all_to_all | solution.py:84
  255.0 4.3 all-to-all-start.1
  259.9 4.3 reduce.1
  268.0 16.8 %all-to-all-done.1 = f32[8,1,32768]{2,1,0:T(1,128)} async-done(((f32[8,1,32768]{2,1,0:T(1,128)}), f32[8,1,32768]{2,1,0:T(1,128)}, u32[]{:S(2)}, u32[]{:S(2)}) %all-to-all-start.1) | async-done | bytes 1048608 | tf_op jit(solution)/shard_map/all_to_all | solution.py:85
  284.9 4.3 reduce
  296.5 4.3 broadcast.389.clone
  300.8 152.3 %while.40 = (s32[]{:T(128)}, f32[8,256,1024]{2,1,0:T(8,128)}, s32[8]{0:T(128)S(1)}, f32[512,1024]{1,0:T(8,128)}, s32[]{:T(128)}, /*index=5*/s32[]{:T(128)}) while((s32[]{:T(128)}, f32[8,256,1024]{2,1,0:T(8,128)}, s32[8]{0:T(128)S(1)}, f32[512,1024]{1,0:T(8,128)}, s32[]{:T(128)}, /*index=5*/s32[]{:T(128)}) %tuple.103), condition=%wide.region_3.4_spmd.clone, body=%wide.region_2.3_spmd.clone.sunk | while | flops 3224116480 | bytes 19929688 | solution.py:108
  304.3 5.1 fusion.91
  323.2 5.1 fusion.91
  342.2 5.1 fusion.91
  361.2 5.1 fusion.91
  380.3 5.1 fusion.91
  399.3 5.1 fusion.91
  418.3 5.1 fusion.91
  437.3 5.1 fusion.91
  453.1 9.2 copy.70
  462.3 70.2 %reduce-scatter.3.cloned.1.call-done = f32[512,1024]{0,1:T(8,128)} async-done(((f32[2048,1024]{0,1:T(8,128)}), f32[512,1024]{0,1:T(8,128)}) %reduce-scatter.3.cloned.1.call-update) | async-done | bytes 2097168 | tf_op jit(solution)/shard_map/reduce_scatter | solution.py:107
  534.0 45.9 %collective-permute-done = f32[512,1024]{0,1:T(8,128)S(1)} collective-permute-done((f32[512,1024]{0,1:T(8,128)}, f32[512,1024]{0,1:T(8,128)S(1)}, u32[]{:S(2)}, u32[]{:S(2)}) %collective-permute-start) | collective-permute-done | bytes 2097184 | tf_op jit(solution)/shard_map/ppermute | solution.py:18
  581.4 44.9 %collective-permute-done.1 = f32[512,1024]{0,1:T(8,128)} collective-permute-done((f32[512,1024]{0,1:T(8,128)S(1)}, f32[512,1024]{0,1:T(8,128)}, u32[]{:S(2)}, u32[]{:S(2)}) %collective-permute-start.1) | collective-permute-done | bytes 2097184 | tf_op jit(solution)/shard_map/ppermute | solution.py:18
  630.4 87.5 %collective-permute-done.2 = f32[512,1024]{0,1:T(8,128)S(1)} collective-permute-done((f32[512,1024]{0,1:T(8,128)}, f32[512,1024]{0,1:T(8,128)S(1)}, u32[]{:S(2)}, u32[]{:S(2)}) %collective-permute-start.2) | collective-permute-done | bytes 2097184 | tf_op jit(solution)/shard_map/ppermute | solution.py:18
  717.9 10.5 %rev.8 = f32[512,2,2,256]{0,3,2,1:T(8,128)} reverse(f32[512,2,2,256]{0,3,2,1:T(8,128)S(1)} %bitcast.107), dimensions={3} | reverse | bytes 4194304 | tf_op jit(solution)/shard_map/jit(_flip)/rev | solution.py:117
  730.9 11.7 %rev.9 = f32[512,2,2,256]{0,3,2,1:T(8,128)} reverse(f32[512,2,2,256]{0,3,2,1:T(8,128)S(1)} %broadcast_select_fusion), dimensions={0} | reverse | bytes 4194304 | tf_op jit(solution)/shard_map/jit(_flip)/rev | solution.py:120
  754.7 4.3 broadcast.389
  759.0 136.0 %while.41 = (s32[]{:T(128)}, f32[8,256,1024]{2,1,0:T(8,128)}, s32[8]{0:T(128)S(1)}, f32[512,1024]{1,0:T(8,128)}, s32[]{:T(128)}, /*index=5*/s32[]{:T(128)}) while((s32[]{:T(128)}, f32[8,256,1024]{2,1,0:T(8,128)}, s32[8]{0:T(128)S(1)}, f32[512,1024]{1,0:T(8,128)}, s32[]{:T(128)}, /*index=5*/s32[]{:T(128)}) %tuple.114), condition=%wide.region_6.7_spmd.clone, body=%wide.region_5.6_spmd.clone.sunk | while | flops 3224123136 | bytes 19929688 | solution.py:158
  762.3 6.5 fusion.97
  779.3 6.5 fusion.97
  796.2 6.5 fusion.97
  813.2 6.5 fusion.97
  830.2 6.5 fusion.97
  847.2 6.5 fusion.97
  864.3 6.5 fusion.97
  881.3 6.5 fusion.97
  895.0 71.6 %reduce-scatter.5.cloned.1.call-done = f32[512,1024]{1,0:T(8,128)} async-done(((f32[2048,1024]{1,0:T(8,128)}), f32[512,1024]{1,0:T(8,128)}) %reduce-scatter.5.cloned.1.call-update) | async-done | bytes 2097168 | tf_op jit(solution)/shard_map/reduce_scatter | solution.py:157
  (245 shorter events, 293.2 us)
Async XLA Ops:
  221.7 7.4 copy-start.2
  221.7 8.1 copy-start.1
  221.7 33.3 %all-to-all-start = ((f32[8,1,32768]{2,1,0:T(1,128)}), f32[8,1,32768]{2,1,0:T(1,128)}, u32[]{:S(2)}, u32[]{:S(2)}) async-start(f32[8,1,32768]{2,1,0:T(1,128)} %reshape.321), calls=%async_computation | async-start | bytes 2097152 | tf_op jit(solution)/shard_map/all_to_all | solution.py:84
  255.0 29.8 %all-to-all-start.1 = ((f32[8,1,32768]{2,1,0:T(1,128)}), f32[8,1,32768]{2,1,0:T(1,128)}, u32[]{:S(2)}, u32[]{:S(2)}) async-start(f32[8,1,32768]{2,1,0:T(1,128)} %reshape.319), calls=%async_computation.1 | async-start | bytes 2097152 | tf_op jit(solution)/shard_map/all_to_all | solution.py:85
  259.3 273.2 %reduce-scatter.3.cloned.1.call-start = ((), (), s32[]{:S(2)}) async-start(), calls=%async_computation.4 | async-start | bytes 10485760 | tf_op jit(solution)/shard_map/reduce_scatter | solution.py:107
  462.3 504.3 %reduce-scatter.5.cloned.1.call-start = ((), (), s32[]{:S(2)}) async-start(), calls=%async_computation.5 | async-start | bytes 10485760 | tf_op jit(solution)/shard_map/reduce_scatter | solution.py:157
  532.5 47.4 %collective-permute-start = (f32[512,1024]{0,1:T(8,128)}, f32[512,1024]{0,1:T(8,128)S(1)}, u32[]{:S(2)}, u32[]{:S(2)}) collective-permute-start(f32[512,1024]{0,1:T(8,128)} %reduce-scatter.3.cloned.1.call-done), channel_id=1, source_target_pairs={{0,1},{1,0},{2,3},{3,2},{4,5},{5,4},{6,7},{7,6},{8,9},{9,8},{10,11... | collective-permute-start | bytes 6291464 | tf_op jit(solution)/shard_map/ppermute | solution.py:18
  579.9 46.4 %collective-permute-start.1 = (f32[512,1024]{0,1:T(8,128)S(1)}, f32[512,1024]{0,1:T(8,128)}, u32[]{:S(2)}, u32[]{:S(2)}) collective-permute-start(f32[512,1024]{0,1:T(8,128)S(1)} %collective-permute-done), channel_id=1, source_target_pairs={{0,2},{2,0},{1,3},{3,1},{4,6},{6,4},{5,7},{7,5},{8,10},{10,8},{9,1... | collective-permute-start | bytes 6291464 | tf_op jit(solution)/shard_map/ppermute | solution.py:18
  626.4 91.5 %collective-permute-start.2 = (f32[512,1024]{0,1:T(8,128)}, f32[512,1024]{0,1:T(8,128)S(1)}, u32[]{:S(2)}, u32[]{:S(2)}) collective-permute-start(f32[512,1024]{0,1:T(8,128)} %collective-permute-done.1), channel_id=1, source_target_pairs={{0,4},{4,0},{1,5},{5,1},{2,6},{6,2},{3,7},{7,3},{8,12},{12,8},{9,1... | collective-permute-start | bytes 6291464 | tf_op jit(solution)/shard_map/ppermute | solution.py:18
  742.6 2.2 copy-start
Sparse Core Ops, SparseCore 0:
  462.4 70.0 reduce-scatter.2
  895.2 71.4 reduce-scatter.4
where the time goes:
time: 989 us; the launch traced here: 978 us
  waiting for transfers between devices  355 us (36%)
  local copies, waits for them, and re-layouts  199 us (20%)
  other arithmetic  196 us (20%)
  matrix products  163 us (16%)
  loops' own time  34.1 us (3%)
  starting transfers between devices  17.2 us (2%)
  between operations  14 us (1%)
    ppermute x3, waiting for transfers between devices, partner_2(): return lax.ppermute(block, axis, route)  178 us
    cos x32, other arithmetic, twiddle(): return (jnp.cos(angles), jnp.sin(angles))  99.5 us
    reduce_scatter x1, waiting for transfers between devices, on_device(): lax.psum_scatter(lax.map(inverse_block_term, offsets).reshape(group_rows...  71.6 us
    reduce_scatter x1, waiting for transfers between devices, on_device(): lax.psum_scatter(lax.map(forward_block_term, offsets).reshape(group_rows...  70.2 us
    dot_general x16, matrix products, row_block(): jnp.dot(stacked, tables, precision=exact_mode, preferred_element_type=jnp...  69.4 us
    dot_general x8, matrix products, inverse_block_term(): jnp.dot(left_side, back_side, precision=exact_mode, preferred_element_typ...  52.1 us
    dot_general x8, matrix products, forward_block_term(): jnp.dot(left_side, right_side, precision=exact_mode, preferred_element_ty...  41.1 us
    another operation x1, loops' own time, on_device(): lax.map(row_block, jnp.arange(block_count, dtype=jnp.int32) * block_width)  33.2 us
  transfers between devices with their start and end apart: 7, of which 7 were waited for; matrix products, arithmetic and copies ran while one was open for 2% of the time, Pallas kernels for 0%

commit v1 on v0

v1 whole, which is shorter than its diff:
```python
import functools
import math

import jax
import jax.numpy as jnp
import numpy as np
from jax import lax
from jax.experimental import pallas as pl
from jax.experimental.pallas import tpu as pltpu
from jax.sharding import PartitionSpec as P


f32 = jnp.float32
bf16 = jnp.bfloat16


def split_two(x):
    high = x.astype(bf16)
    return high, (x - high.astype(f32)).astype(bf16)


def split_three(x):
    high = x.astype(bf16)
    rest = x - high.astype(f32)
    middle = rest.astype(bf16)
    return high, middle, (rest - middle.astype(f32)).astype(bf16)


def dot(a, b):
    return jnp.dot(a, b, preferred_element_type=f32)


def signed_scale(waves, length):
    signed = jnp.where(waves < length // 2, waves, waves - length)
    signed = jnp.where(waves == length // 2, 0, signed)
    return 2.0 / length * signed.astype(f32)


def cos_sin(residue, length):
    eighth = length // 8
    turned = (residue + eighth) & (length - 1)
    turn = turned // (2 * eighth)
    x = (2.0 * math.pi / length) * (turned - turn * (2 * eighth) - eighth).astype(f32)
    y = x * x
    cosine = 1.0 + y * (-1 / 2 + y * (1 / 24 + y * (-1 / 720 + y * (1 / 40320))))
    sine = x * (1.0 + y * (-1 / 6 + y * (1 / 120 + y * (-1 / 5040 + y * (1 / 362880)))))
    odd = (turn & 1) == 1
    first, second = jnp.where(odd, sine, cosine), jnp.where(odd, cosine, sine)
    return (
        jnp.where((turn == 1) | (turn == 2), -first, first),
        jnp.where(turn >= 2, -second, second),
    )


def reverse_lanes(x, swap):
    high, middle, low = split_three(x)
    return dot(high, swap) + (dot(middle, swap) + dot(low, swap))


def transform_block(fields, table_ref, waves, first, slab):
    field_high, field_low = fields
    rows = field_high.shape[0] // 4
    half = table_ref.shape[2] // 2
    sums = []
    for part in range(2):
        columns = pl.ds(part * half + first, slab)
        high, low = table_ref[0, :, columns], table_ref[1, :, columns]
        sums.append(dot(field_high, high) + (dot(field_high, low) + dot(field_low, high)))
    residue = waves & 3
    sign = jnp.where((residue & 1) == 1, -1.0, 1.0)
    cosine = jnp.where(residue == 0, 1.0, jnp.where(residue == 2, -1.0, 0.0))
    sine = jnp.where(residue == 1, 1.0, jnp.where(residue == 3, -1.0, 0.0))

    def folded(x):
        return (
            x[:rows] + sign * x[2 * rows : 3 * rows],
            x[rows : 2 * rows] + sign * x[3 * rows :],
        )

    even_c, odd_c = folded(sums[0])
    even_s, odd_s = folded(sums[1])
    return (
        even_c + cosine * odd_c - sine * odd_s,
        even_s + cosine * odd_s + sine * odd_c,
    )


def fill_table(waves, table_ref):
    half = waves.shape[1]
    length = 2 * half
    norm = 1.0 / math.sqrt(length)
    fine = 32
    coarse = length // 4 // fine
    special = (waves == 0) | (waves == half)
    coarse_c, coarse_s = cos_sin(
        (fine * lax.broadcasted_iota(jnp.int32, (coarse, half), 0) * waves) & (length - 1), length
    )
    coarse_c, coarse_s = norm * coarse_c, norm * coarse_s
    index = lax.broadcasted_iota(jnp.int32, (fine, half), 0)
    fine_c, fine_s = cos_sin((index * waves) & (length - 1), length)
    other = norm * jnp.where((waves == 0) & ((index & 1) == 1), -1.0, 1.0)
    for a in range(coarse):
        this_c, this_s = coarse_c[a : a + 1], coarse_s[a : a + 1]
        here = slice(a * fine, (a + 1) * fine)
        cosines = this_c * fine_c - this_s * fine_s
        sines = this_c * fine_s + this_s * fine_c
        sines = jnp.where(special, other, sines)
        for part, values in enumerate((cosines, sines)):
            high, low = split_two(values)
            table_ref[0, here, part * half : (part + 1) * half] = high
            table_ref[1, here, part * half : (part + 1) * half] = low


def load_quarters(ref):
    quarter = ref.shape[1] // 4
    x = jnp.concatenate([ref[:, i * quarter : (i + 1) * quarter] for i in range(4)], 0)
    return split_two(x)


def second_kernel(sizes, order_ref, field_hbm, out_hbm, field_ref, table_ref, piece_ref, sems):
    planes, rows, slab, pens = sizes
    load = pltpu.make_async_copy(field_hbm, field_ref, sems.at[pens])
    load.start()
    half = order_ref.shape[1] // 2
    fill_table(order_ref[:, :half], table_ref)
    load.wait()
    fields = load_quarters(field_ref)
    copies = []
    for block in range(pens // 2):
        here = slice(block * slab, (block + 1) * slab)
        c, s = transform_block(fields, table_ref, order_ref[:, here], block * slab, slab)
        for part, values in enumerate((s, c)):
            for plane in range(planes):
                piece_ref[block, part * planes + plane] = values[plane * rows : (plane + 1) * rows]
        for target in (block, pens - 1 - block):
            copy = pltpu.make_async_copy(
                piece_ref.at[block], out_hbm.at[:, target], sems.at[target]
            )
            copy.start()
            copies.append(copy)
    for copy in copies:
        copy.wait()


def first_kernel(sizes, place_ref, order_ref, swap_ref, field_hbm, *refs):
    planes, rows, slab, pens = sizes
    outs, (field_ref, table_ref, piece_ref, sems) = refs[:pens], refs[pens:]
    load = pltpu.make_async_copy(field_hbm, field_ref, sems.at[pens])
    load.start()
    length = order_ref.shape[1]
    fill_table(order_ref[:, : length // 2], table_ref)
    load.wait()
    fields = load_quarters(field_ref)
    pen = place_ref[0]
    upper = pen >= pens // 2
    lanes = 128
    step = 2 * planes * (slab // lanes)
    copies = []
    for slot in range(pens // 2):
        target = pen ^ slot
        block = jnp.where(upper, pens - 1 - target, target)
        first = pl.multiple_of(block * slab, slab)
        waves = order_ref[:, pl.ds(first, slab)]
        c, s = transform_block(fields, table_ref, waves, first, slab)
        scale = signed_scale(waves, length)
        opposite = slot ^ (pens - 1)
        for part, values in enumerate((scale * s, scale * c)):
            turned = reverse_lanes(values, swap_ref[...])
            if part == 1:
                turned = -turned
            near, far = jnp.where(upper, turned, values), jnp.where(upper, values, turned)
            for to, piece in ((slot, near), (opposite, far)):
                for plane in range(planes):
                    for tile in range(slab // lanes):
                        at = (part * (slab // lanes) + tile) * planes + plane
                        piece_ref[to, pl.ds(at, rows, stride=step), :] = piece[
                            plane * rows : (plane + 1) * rows, tile * lanes : (tile + 1) * lanes
                        ]
        for to in (slot, opposite):
            copy = pltpu.make_async_copy(piece_ref.at[to], outs[to], sems.at[to])
            copy.start()
            copies.append(copy)
    for copy in copies:
        copy.wait()


def table_kernel(after_ref, out_ref):
    half = out_ref.shape[1]
    length = 2 * half
    width = half // 4
    rows = 64
    for distance in range(4):
        for at in range(0, width, rows):
            n = (
                lax.broadcasted_iota(jnp.int32, (rows, width), 0)
                - lax.broadcasted_iota(jnp.int32, (rows, width), 1)
                + (distance * width + at)
            )
            cosine, sine = cos_sin(n & (length - 1), length)
            factor = jnp.where((n & 1) == 1, 1.0 / length, -1.0 / length)
            inverse = jnp.where(n == 0, 0.0, factor / jnp.where(n == 0, 1.0, sine))
            parts = split_two(cosine * inverse) + split_two(inverse)
            for column in range(4):
                row = (column + distance) % 4
                for i, part in enumerate(parts):
                    wrapped = i >= 2 and row < column
                    out_ref[
                        i,
                        row * width + at : row * width + at + rows,
                        column * width : (column + 1) * width,
                    ] = -part if wrapped else part


def circulant_kernel(pair, place_ref, recv_ref, table_ref, turn_ref, near_ref, far_ref):
    group = place_ref[1] ^ pair
    half = recv_ref.shape[0] // 2
    top, bottom = recv_ref[:half, :], recv_ref[half:, :]
    turn = turn_ref[...]

    def operands(x):
        return [dot(part, turn).astype(bf16) for part in split_two(x)]

    plus, minus = operands(top + bottom), operands(top - bottom)
    count = half // 2
    first = pl.multiple_of((group & 1) * count, count)
    swapped = group >= 2
    rows = 256
    for at in range(0, count, rows):
        here = pl.ds(first + at, rows)

        def product(which, high, low):
            return dot(table_ref[2 * which, here, :], high) + (
                dot(table_ref[2 * which, here, :], low) + dot(table_ref[2 * which + 1, here, :], high)
            )

        even, odd = product(0, *plus), product(1, *minus)
        near_ref[at : at + rows, :] = even + jnp.where(swapped, -odd, odd)
        far_ref[at : at + rows, :] = even + jnp.where(swapped, odd, -odd)


def final_kernel(sizes, place_ref, mask_ref, *refs):
    planes, rows, slab, pens = sizes
    firsts, seconds, out_hbm = refs[:pens], refs[pens : pens + 4], refs[pens + 4]
    first_ref, second_ref, piece_ref, sems = refs[pens + 5 :]
    lanes = 128
    tiles = slab // lanes
    step = 2 * planes * tiles
    loads = [
        pltpu.make_async_copy(ref, second_ref.at[k], sems.at[2 * pens + k])
        for k, ref in enumerate(seconds)
    ] + [
        pltpu.make_async_copy(ref, first_ref.at[k], sems.at[k]) for k, ref in enumerate(firsts)
    ]
    for load in loads:
        load.start()
    pen, group = place_ref[0], place_ref[1]
    upper = pen >= pens // 2
    low_bit, high_bit = (group & 1) == 1, group >= 2
    special = mask_ref[...] > 0.0
    for load in loads[:4]:
        load.wait()
    stores = []
    for slot in range(pens):
        source = pen ^ slot
        here = pl.ds(pl.multiple_of(source * rows, rows), rows)
        r = [second_ref[k, here, :] for k in range(4)]
        r = [jnp.where(low_bit, r[k ^ 1], r[k]) for k in range(4)]
        r = [jnp.where(high_bit, r[k ^ 2], r[k]) for k in range(4)]
        loads[4 + slot].wait()
        for plane in range(planes):
            s, c = r[plane], r[planes + plane]
            pieces = (
                jnp.where(special, 0.0, jnp.where(upper, s, -s)),
                jnp.where(special & upper, -s, -c),
            )
            for part in range(2):
                for tile in range(tiles):
                    there = pl.ds((part * tiles + tile) * planes + plane, rows, stride=step)
                    piece_ref[slot, there, :] = (
                        first_ref[slot, there, :]
                        + pieces[part][:, tile * lanes : (tile + 1) * lanes]
                    )
        size = rows * step
        store = pltpu.make_async_copy(
            piece_ref.at[slot],
            out_hbm.at[pl.ds(pl.multiple_of(source * size, size), size)],
            sems.at[pens + slot],
        )
        store.start()
        stores.append(store)
    for store in stores:
        store.wait()


SPACES = {"s": pltpu.SMEM, "v": pltpu.VMEM, "h": pltpu.HBM, "a": pl.ANY}


def kernel_call(body, shapes, spaces, flops, moved, limit, scratch=()):
    inputs, outputs = spaces.split(">")
    specs = [pl.BlockSpec(memory_space=SPACES[s]) for s in outputs]
    return pl.pallas_call(
        body,
        out_shape=shapes,
        in_specs=[pl.BlockSpec(memory_space=SPACES[s]) for s in inputs],
        out_specs=specs if isinstance(shapes, list) else specs[0],
        scratch_shapes=scratch,
        cost_estimate=pl.CostEstimate(flops=flops, bytes_accessed=moved, transcendentals=0),
        compiler_params=pltpu.CompilerParams(vmem_limit_bytes=limit * 2**20),
    )


def exchange(block, axis, distance):
    size = lax.axis_size(axis)
    return lax.ppermute(block, axis, [(i, i ^ distance) for i in range(size)])


def fast_path(u, v, ky_order, sizes, groups):
    planes, rows, slab, pens = sizes
    length_y = v.shape[1]
    group_rows = rows * pens
    length_z = group_rows * groups
    half = length_y // 2
    lanes = 128
    pen, group = lax.axis_index("pen"), lax.axis_index("grp")
    place = jnp.stack([pen, group]).astype(jnp.int32)
    order = ky_order[None, :]
    flops = 2 * 3 * planes * rows * length_y * length_y
    dma = pltpu.SemaphoreType.DMA
    field = pltpu.VMEM(v.shape, f32)
    table = pltpu.VMEM((2, length_y // 4, length_y), bf16)
    v_blocks = kernel_call(
        functools.partial(second_kernel, sizes),
        jax.ShapeDtypeStruct((2 * planes, pens, rows, slab), f32),
        "vh>h",
        flops,
        2**22,
        60,
        [field, table, pltpu.VMEM((pens // 2, 2 * planes, rows, slab), f32), dma((pens + 1,))],
    )(order, v)
    recv = lax.all_to_all(
        v_blocks.reshape(groups * pens, rows, slab), ("grp", "pen"), 0, 0, tiled=True
    ).reshape(length_z, slab)
    swap = jnp.asarray(np.eye(slab)[::-1].copy(), bf16)
    size = rows * 2 * planes * slab // lanes
    firsts = kernel_call(
        functools.partial(first_kernel, sizes),
        [jax.ShapeDtypeStruct((size, lanes), f32)] * pens,
        "svvh>" + "h" * pens,
        flops,
        2**22,
        60,
        [field, table, pltpu.VMEM((pens, size, lanes), f32), dma((pens + 1,))],
    )(place, order, swap, u)
    circulant = kernel_call(
        table_kernel,
        jax.ShapeDtypeStruct((4, length_z // 2, length_z // 2), bf16),
        "a>v",
        2**24,
        2**23,
        16,
    )(firsts[0])
    arrived = {0: firsts[0]}
    for k in reversed(range(1, pens)):
        arrived[k] = exchange(firsts[k], "pen", k)
    turn = jnp.where(pen >= pens // 2, swap, jnp.asarray(np.eye(slab), bf16))
    seconds = [None] * groups
    for pair in range(2):
        both = kernel_call(
            functools.partial(circulant_kernel, pair),
            [jax.ShapeDtypeStruct((group_rows, slab), f32)] * 2,
            "svvv>vv",
            3 * length_z * length_z * slab // 2,
            2**23,
            20,
        )(place, recv, circulant, turn)
        for k, values in zip((pair, pair + 2), both):
            seconds[k] = exchange(values, "grp", k) if k else values
    mine = lax.dynamic_slice_in_dim(ky_order, pen * slab, slab)
    special = ((mine == 0) | (mine == half)).astype(f32)[None, :]
    result = kernel_call(
        functools.partial(final_kernel, sizes),
        jax.ShapeDtypeStruct((pens * size, lanes), f32),
        "sv" + "a" * (pens + groups) + ">h",
        2**23,
        2**22,
        16,
        [
            pltpu.VMEM((pens, size, lanes), f32),
            pltpu.VMEM((groups, group_rows, slab), f32),
            pltpu.VMEM((pens, size, lanes), f32),
            dma((2 * pens + groups,)),
        ],
    )(place, special, *[arrived[k] for k in range(pens)], *seconds)
    result = result.reshape(group_rows, 2, slab // lanes, planes, lanes)
    return jnp.transpose(result, (0, 1, 3, 2, 4)).reshape(group_rows, 2, planes, slab)


def whole_tables(length):
    half = length // 2
    n = lax.broadcasted_iota(jnp.int32, (half, half), 0) - lax.broadcasted_iota(
        jnp.int32, (half, half), 1
    )
    theta = 2.0 * math.pi / length * n.astype(f32)
    factor = jnp.where(n % 2 == 0, -1.0 / length, 1.0 / length)
    inverse = jnp.where(n == 0, 0.0, factor / jnp.where(n == 0, 1.0, jnp.sin(theta)))
    return jnp.cos(theta) * inverse, inverse


def plain_path(u, v, ky_order, sizes, groups):
    planes, rows, slab, pens = sizes
    length_y = v.shape[1]
    group_rows = rows * pens
    length_z = group_rows * groups
    half = length_y // 2
    exact = lax.Precision.HIGHEST
    pen = lax.axis_index("pen")
    upper = pen >= pens // 2
    waves = ky_order[:half]
    index = lax.iota(jnp.int32, length_y)[:, None]
    theta = 2.0 * math.pi / length_y * (index * waves[None, :] % length_y).astype(f32)
    mixed = 2.0 * math.pi / length_y * (index * (half - waves[None, :]) % length_y).astype(f32)
    special = (waves == 0) | (waves == half)
    sines = jnp.where(special, jnp.cos(mixed), jnp.sin(theta))
    both = 1.0 / math.sqrt(length_y) * jnp.stack([sines, jnp.cos(theta)])

    def transform(x):
        y = jnp.einsum("ry,pyk->prk", x, both, precision=exact)
        return y.reshape(2, planes, rows, pens // 2, slab)

    y = transform(v)
    y = jnp.concatenate([y, jnp.flip(y, 3)], 3)
    v_blocks = jnp.transpose(y, (3, 2, 0, 1, 4)).reshape(pens, rows, groups, -1)
    v_blocks = jnp.transpose(v_blocks, (2, 0, 1, 3)).reshape(groups * pens, rows, -1)
    y = transform(u) * signed_scale(waves, length_y).reshape(pens // 2, slab)
    turned = jnp.flip(y, (3, 4)) * jnp.array([1.0, -1.0], f32)[:, None, None, None, None]
    u_blocks = jnp.transpose(jnp.concatenate([y, turned], 3), (3, 2, 0, 1, 4))
    recv = lax.all_to_all(v_blocks, ("grp", "pen"), 0, 0, tiled=True).reshape(length_z, -1)
    u_recv = lax.all_to_all(u_blocks, "pen", 0, 0, tiled=True)
    table = whole_tables(length_z)
    top, bottom = recv[: length_z // 2], recv[length_z // 2 :]
    even = jnp.dot(table[0], top + bottom, precision=exact)
    odd = jnp.dot(table[1], top - bottom, precision=exact)
    deriv = jnp.concatenate([even + odd, even - odd], 0)
    back = lax.all_to_all(deriv.reshape(groups, group_rows, -1), "grp", 0, 0, tiled=True)
    back = jnp.transpose(back, (1, 0, 2)).reshape(group_rows, 2, planes, slab)
    back = jnp.where(upper, jnp.flip(back, 3), back)
    mine = lax.dynamic_slice_in_dim(ky_order, pen * slab, slab)
    special = (mine == 0) | (mine == half)
    s, c = back[:, 0], back[:, 1]
    first = jnp.where(special, 0.0, jnp.where(upper, s, -s))
    second = jnp.where(special & upper, -s, -c)
    return u_recv.reshape(group_rows, 2, planes, slab) + jnp.stack([first, second], 1)


def on_device(u_field, v_field, ky_order):
    planes, rows, length_y = u_field.shape
    pens, groups = lax.axis_size("pen"), lax.axis_size("grp")
    slab = length_y // pens
    u = u_field.reshape(planes * rows, length_y)
    v = v_field.reshape(planes * rows, length_y)
    fast = slab % 128 == 0 and rows % 8 == 0 and groups == 4 and planes == 2 and pens % 4 == 0
    fast = fast and length_y % 1024 == 0 and length_y & (length_y - 1) == 0 and pens & (pens - 1) == 0
    path = fast_path if fast else plain_path
    return path(u, v, ky_order, (planes, rows, slab, pens), groups)


def solution(mesh):
    placed = (P(None, ("grp", "pen"), None), P(None, ("grp", "pen"), None), P())

    return jax.shard_map(
        on_device,
        mesh=mesh,
        in_specs=placed,
        out_specs=P("grp", None, None, "pen"),
        check_vma=False,
    )
```

time: 989 us -> 110 us (0.11)
  the two profiles are of different devices: /device:TPU:0 before, /device:TPU:8 now
where the time goes in v1:
time: 110 us
  waiting for transfers between devices  51.8 us (47%)
  Pallas kernels  28 us (25%)
  starting transfers between devices  20.5 us (19%)
  local copies, waits for them, and re-layouts  7.58 us (7%)
  other arithmetic  1.38 us (1%)
    all_to_all x1, waiting for transfers between devices, fast_path(): lax.all_to_all(v_blocks.reshape(groups * pens, rows, slab), ('grp', 'pen'...  26.3 us
    ppermute x10, waiting for transfers between devices, exchange(): return lax.ppermute(block, axis, [(i, i ^ distance) for i in range(size)])  25.5 us
    ppermute x10, starting transfers between devices, exchange(): return lax.ppermute(block, axis, [(i, i ^ distance) for i in range(size)])  14.3 us
    pallas_call x1, Pallas kernels, fast_path(): kernel_call(functools.partial(first_kernel, sizes), [jax.ShapeDtypeStruct...  8.02 us
    pallas_call x2, Pallas kernels, fast_path(): kernel_call(functools.partial(circulant_kernel, pair), [jax.ShapeDtypeStr...  7.6 us
    unnamed x14, local copies, waits for them, and re-layouts  7.58 us
    pallas_call x1, Pallas kernels, fast_path(): kernel_call(functools.partial(second_kernel, sizes), jax.ShapeDtypeStruct...  6.71 us
    all_to_all x1, starting transfers between devices, fast_path(): lax.all_to_all(v_blocks.reshape(groups * pens, rows, slab), ('grp', 'pen'...  6.23 us
  transfers between devices with their start and end apart: 11, of which 5 were waited for; matrix products, arithmetic and copies ran while one was open for 1% of the time, Pallas kernels for 17%

profile of v1, /device:TPU:8, one launch (start us, length us, event | category | flops | bytes accessed | tf_op | source)
XLA Modules:
  0.0 109.5 jit_solution(2370293126687023039)
XLA Ops:
  0.0 6.7 %shard_map.56 = f32[4,8,64,256]{3,2,1,0:T(8,128)} custom-call(s32[1,2048]{1,0:T(1,128)} %bitcast.17, f32[128,2048]{1,0:T(8,128)} %bitcast.19), custom_call_target="tpu_custom_call" | custom-call | flops 3221225472 | bytes 4194304 | tf_op jit(solution)/shard_map/pallas_call | solution.py:331
  6.7 6.2 %all-to-all-start = ((f32[32,64,256]{2,1,0:T(8,128)}), f32[32,64,256]{2,1,0:T(8,128)S(1)}, u32[]{:S(2)}, u32[]{:S(2)}) async-start(f32[32,64,256]{2,1,0:T(8,128)} %bitcast.16), calls=%async_computation | async-start | bytes 4194304 | tf_op jit(solution)/shard_map/all_to_all | solution.py:340
  13.0 0.6 pad_add_fusion.place_ref
  13.6 8.0 %shard_map.55 = (f32[512,128]{1,0:T(8,128)}, f32[512,128]{1,0:T(8,128)}, f32[512,128]{1,0:T(8,128)}, f32[512,128]{1,0:T(8,128)}, f32[512,128]{1,0:T(8,128)}, /*i...) custom-call(s32[2]{0:T(128)} %pad_add_fusion.place_ref, s32[1,2048]{1,0:T(1,128)} %bitcast.18, ...), custom_call_target="tpu_custom_call" | custom-call | flops 3221225472 | bytes 4194304 | tf_op jit(solution)/shard_map/pallas_call | solution.py:345
  21.6 1.5 %collective-permute-start = (f32[512,128]{1,0:T(8,128)}, f32[512,128]{1,0:T(8,128)S(1)}, u32[]{:S(2)}, u32[]{:S(2)}) collective-permute-start(f32[512,128]{1,0:T(8,128)} %get-tuple-element.18), channel_id=1, source_target_pairs={{0,1},{1,0},{2,3},{3,2},{4,5},{5,4},{6,7},{7,6},{8,9},{9,8},{10,11... | collective-permute-start | bytes 786440 | tf_op jit(solution)/shard_map/ppermute | solution.py:314
  23.1 0.6 collective-permute-start.1
  23.7 1.5 %collective-permute-start.2 = (f32[512,128]{1,0:T(8,128)}, f32[512,128]{1,0:T(8,128)}, u32[]{:S(2)}, u32[]{:S(2)}) collective-permute-start(f32[512,128]{1,0:T(8,128)} %get-tuple-element.20), channel_id=1, source_target_pairs={{0,3},{1,2},{2,1},{3,0},{4,7},{5,6},{6,5},{7,4},{8,11},{9,10},{10,... | collective-permute-start | bytes 786440 | tf_op jit(solution)/shard_map/ppermute | solution.py:314
  25.2 2.4 %collective-permute-start.3 = (f32[512,128]{1,0:T(8,128)}, f32[512,128]{1,0:T(8,128)}, u32[]{:S(2)}, u32[]{:S(2)}) collective-permute-start(f32[512,128]{1,0:T(8,128)} %get-tuple-element.21), channel_id=1, source_target_pairs={{0,4},{1,5},{2,6},{3,7},{4,0},{5,1},{6,2},{7,3},{8,12},{9,13},{10,... | collective-permute-start | bytes 786440 | tf_op jit(solution)/shard_map/ppermute | solution.py:314
  27.6 1.4 %collective-permute-start.4 = (f32[512,128]{1,0:T(8,128)}, f32[512,128]{1,0:T(8,128)}, u32[]{:S(2)}, u32[]{:S(2)}) collective-permute-start(f32[512,128]{1,0:T(8,128)} %get-tuple-element.22), channel_id=1, source_target_pairs={{0,5},{1,4},{2,7},{3,6},{4,1},{5,0},{6,3},{7,2},{8,13},{9,12},{10,... | collective-permute-start | bytes 786440 | tf_op jit(solution)/shard_map/ppermute | solution.py:314
  29.0 0.0 copy-start.2
  29.0 0.9 copy-done.2
  29.9 0.0 copy-start.5
  29.9 0.0 copy-start.6
  29.9 0.0 copy-start.4
  29.9 2.5 %shard_map.57.table_ref = bf16[4,1024,1024]{2,1,0:T(8,128)(2,1)S(1)} custom-call(f32[512,128]{1,0:T(8,128)S(1)} %copy-done.2), custom_call_target="tpu_custom_call" | custom-call | flops 16777216 | bytes 8388608 | tf_op jit(solution)/shard_map/pallas_call | solution.py:354
  32.4 0.0 copy-start
  32.4 3.2 %copy-done = bf16[4,1024,1024]{2,1,0:T(8,128)(2,1)} copy-done((bf16[4,1024,1024]{2,1,0:T(8,128)(2,1)}, bf16[4,1024,1024]{2,1,0:T(8,128)(2,1)S(1)}, u32[]{:S(2)}) %copy-start) | copy-done | bytes 8388632
  35.7 0.0 copy-done.5
  35.7 0.0 copy-done.6
  35.7 26.3 %all-to-all-done = f32[32,64,256]{2,1,0:T(8,128)S(1)} async-done(((f32[32,64,256]{2,1,0:T(8,128)}), f32[32,64,256]{2,1,0:T(8,128)S(1)}, u32[]{:S(2)}, u32[]{:S(2)}) %all-to-all-start) | async-done | bytes 2097184 | tf_op jit(solution)/shard_map/all_to_all | solution.py:340
  62.0 0.0 copy-done.4
  62.0 0.0 copy-start.1
  62.0 3.4 %copy-done.1 = bf16[4,1024,1024]{2,1,0:T(8,128)(2,1)S(1)} copy-done((bf16[4,1024,1024]{2,1,0:T(8,128)(2,1)S(1)}, bf16[4,1024,1024]{2,1,0:T(8,128)(2,1)}, u32[]{:S(2)}) %copy-start.1) | copy-done | bytes 8388632
  65.4 3.9 %shard_map.59 = (f32[512,256]{1,0:T(8,128)}, f32[512,256]{1,0:T(8,128)}) custom-call(s32[2]{0:T(128)S(1)} %copy-done.4, f32[2048,256]{1,0:T(8,128)S(1)} %bitcast.13, bf16[4,1024,1024]{2,1,0:T(8,128)(2,1)S(1)} %copy-done.1, bf16[256,256]{1,0:T(8,128)(2,1)S(1)} %broadcast_select_fusion.turn_ref), custom_call_target="tpu_custom_call" | custom-call | flops 1610612736 | bytes 8388608 | tf_op jit(solution)/shard_map/pallas_call | solution.py:368
  69.3 0.0 copy-start.3
  69.3 3.7 %shard_map.58 = (f32[512,256]{1,0:T(8,128)S(1)}, f32[512,256]{1,0:T(8,128)}) custom-call(s32[2]{0:T(128)S(1)} %copy-done.4, f32[2048,256]{1,0:T(8,128)S(1)} %bitcast.14, bf16[4,1024,1024]{2,1,0:T(8,128)(2,1)S(1)} %copy-done.1, bf16[256,256]{1,0:T(8,128)(2,1)S(1)} %broadcast_select_fusion.turn_ref), custom_call_target="tpu_custom_call" | custom-call | flops 1610612736 | bytes 8388608 | tf_op jit(solution)/shard_map/pallas_call | solution.py:368
  73.0 0.0 collective-permute-done.refs_1_
  73.0 1.0 collective-permute-start.7
  74.0 0.0 collective-permute-done.1.refs_2_
  74.0 0.4 collective-permute-start.9
  74.4 0.0 collective-permute-done.2.refs_3_
  74.4 1.3 %collective-permute-start.8 = (f32[512,256]{1,0:T(8,128)}, f32[512,256]{1,0:T(8,128)S(1)}, u32[]{:S(2)}, u32[]{:S(2)}) collective-permute-start(f32[512,256]{1,0:T(8,128)} %get-tuple-element.27), channel_id=1, source_target_pairs={{0,16},{8,24},{16,0},{24,8},{1,17},{9,25},{17,1},{25,9},{2,18},{10... | collective-permute-start | bytes 1572872 | tf_op jit(solution)/shard_map/ppermute | solution.py:314
  75.7 0.1 collective-permute-done.3.refs_4_
  75.8 1.7 %collective-permute-start.5 = (f32[512,128]{1,0:T(8,128)}, f32[512,128]{1,0:T(8,128)S(1)}, u32[]{:S(2)}, u32[]{:S(2)}) collective-permute-start(f32[512,128]{1,0:T(8,128)} %get-tuple-element.23), channel_id=1, source_target_pairs={{0,6},{1,7},{2,4},{3,5},{4,2},{5,3},{6,0},{7,1},{8,14},{9,15},{10,... | collective-permute-start | bytes 786440 | tf_op jit(solution)/shard_map/ppermute | solution.py:314
  77.5 9.5 %collective-permute-done.4.refs_5_ = f32[512,128]{1,0:T(8,128)} collective-permute-done((f32[512,128]{1,0:T(8,128)}, f32[512,128]{1,0:T(8,128)}, u32[]{:S(2)}, u32[]{:S(2)}) %collective-permute-start.4) | collective-permute-done | bytes 262176 | tf_op jit(solution)/shard_map/ppermute | solution.py:314
  87.0 2.5 %collective-permute-start.6 = (f32[512,128]{1,0:T(8,128)}, f32[512,128]{1,0:T(8,128)S(1)}, u32[]{:S(2)}, u32[]{:S(2)}) collective-permute-start(f32[512,128]{1,0:T(8,128)} %get-tuple-element.24), channel_id=1, source_target_pairs={{0,7},{1,6},{2,5},{3,4},{4,3},{5,2},{6,1},{7,0},{8,15},{9,14},{10,... | collective-permute-start | bytes 786440 | tf_op jit(solution)/shard_map/ppermute | solution.py:314
  89.5 0.8 or_convert_fusion
  90.3 10.1 %collective-permute-done.5.refs_6_ = f32[512,128]{1,0:T(8,128)S(1)} collective-permute-done((f32[512,128]{1,0:T(8,128)}, f32[512,128]{1,0:T(8,128)S(1)}, u32[]{:S(2)}, u32[]{:S(2)}) %collective-permute-start.5) | collective-permute-done | bytes 262176 | tf_op jit(solution)/shard_map/ppermute | solution.py:314
  100.3 5.8 %collective-permute-done.6.refs_7_ = f32[512,128]{1,0:T(8,128)S(1)} collective-permute-done((f32[512,128]{1,0:T(8,128)}, f32[512,128]{1,0:T(8,128)S(1)}, u32[]{:S(2)}, u32[]{:S(2)}) %collective-permute-start.6) | collective-permute-done | bytes 262176 | tf_op jit(solution)/shard_map/ppermute | solution.py:314
  106.2 0.0 collective-permute-done.7.refs_9_
  106.2 0.0 collective-permute-done.9.refs_11_
  106.2 0.0 collective-permute-done.8.refs_10_
  106.2 0.0 copy-done.3
  106.2 3.2 %shard_map.60 = f32[4096,128]{1,0:T(8,128)} custom-call(s32[2]{0:T(128)S(1)} %copy-done.4, f32[1,256]{1,0:T(1,128)S(1)} %bitcast.15, f32[512,128]{1,0:T(8,128)S(1)} %copy-done.3, f32[512,128]{1,0:T(8,128)S(1)} %collective-permute-done.refs_1_, f32[512,128]{1,0:T(8,128)S(1)} %collective-permute-done.1.refs_2_, f32[512,128]{1,0:T(8,128)} %collective-permute-done.2.refs_3_, ...), custom_call_target="tpu_custom_call" | custom-call | flops 8388608 | bytes 4194304 | tf_op jit(solution)/shard_map/pallas_call | solution.py:380
  (1 shorter events, 0.0 us)
Async XLA Ops:
  6.7 55.3 %all-to-all-start = ((f32[32,64,256]{2,1,0:T(8,128)}), f32[32,64,256]{2,1,0:T(8,128)S(1)}, u32[]{:S(2)}, u32[]{:S(2)}) async-start(f32[32,64,256]{2,1,0:T(8,128)} %bitcast.16), calls=%async_computation | async-start | bytes 4194304 | tf_op jit(solution)/shard_map/all_to_all | solution.py:340
  21.6 51.4 %collective-permute-start = (f32[512,128]{1,0:T(8,128)}, f32[512,128]{1,0:T(8,128)S(1)}, u32[]{:S(2)}, u32[]{:S(2)}) collective-permute-start(f32[512,128]{1,0:T(8,128)} %get-tuple-element.18), channel_id=1, source_target_pairs={{0,1},{1,0},{2,3},{3,2},{4,5},{5,4},{6,7},{7,6},{8,9},{9,8},{10,11... | collective-permute-start | bytes 786440 | tf_op jit(solution)/shard_map/ppermute | solution.py:314
  23.1 50.9 %collective-permute-start.1 = (f32[512,128]{1,0:T(8,128)}, f32[512,128]{1,0:T(8,128)S(1)}, u32[]{:S(2)}, u32[]{:S(2)}) collective-permute-start(f32[512,128]{1,0:T(8,128)} %get-tuple-element.19), channel_id=1, source_target_pairs={{0,2},{1,3},{2,0},{3,1},{4,6},{5,7},{6,4},{7,5},{8,10},{9,11},{10,... | collective-permute-start | bytes 786440 | tf_op jit(solution)/shard_map/ppermute | solution.py:314
  23.7 50.7 %collective-permute-start.2 = (f32[512,128]{1,0:T(8,128)}, f32[512,128]{1,0:T(8,128)}, u32[]{:S(2)}, u32[]{:S(2)}) collective-permute-start(f32[512,128]{1,0:T(8,128)} %get-tuple-element.20), channel_id=1, source_target_pairs={{0,3},{1,2},{2,1},{3,0},{4,7},{5,6},{6,5},{7,4},{8,11},{9,10},{10,... | collective-permute-start | bytes 786440 | tf_op jit(solution)/shard_map/ppermute | solution.py:314
  25.2 50.7 %collective-permute-start.3 = (f32[512,128]{1,0:T(8,128)}, f32[512,128]{1,0:T(8,128)}, u32[]{:S(2)}, u32[]{:S(2)}) collective-permute-start(f32[512,128]{1,0:T(8,128)} %get-tuple-element.21), channel_id=1, source_target_pairs={{0,4},{1,5},{2,6},{3,7},{4,0},{5,1},{6,2},{7,3},{8,12},{9,13},{10,... | collective-permute-start | bytes 786440 | tf_op jit(solution)/shard_map/ppermute | solution.py:314
  27.6 59.5 %collective-permute-start.4 = (f32[512,128]{1,0:T(8,128)}, f32[512,128]{1,0:T(8,128)}, u32[]{:S(2)}, u32[]{:S(2)}) collective-permute-start(f32[512,128]{1,0:T(8,128)} %get-tuple-element.22), channel_id=1, source_target_pairs={{0,5},{1,4},{2,7},{3,6},{4,1},{5,0},{6,3},{7,2},{8,13},{9,12},{10,... | collective-permute-start | bytes 786440 | tf_op jit(solution)/shard_map/ppermute | solution.py:314
  29.0 0.9 copy-start.2
  29.9 5.7 %copy-start.5 = (bf16[256,256]{1,0:T(8,128)(2,1)S(1)}, bf16[256,256]{1,0:T(8,128)(2,1)}, u32[]{:S(2)}) copy-start(bf16[256,256]{1,0:T(8,128)(2,1)} %constant.23.clone.swap_ref) | copy-start | bytes 393220
  29.9 5.7 %copy-start.6 = (bf16[256,256]{1,0:T(8,128)(2,1)S(1)}, bf16[256,256]{1,0:T(8,128)(2,1)}, u32[]{:S(2)}) copy-start(bf16[256,256]{1,0:T(8,128)(2,1)} %constant.24.clone) | copy-start | bytes 393220
  29.9 32.1 %copy-start.4 = (s32[2]{0:T(128)S(1)}, s32[2]{0:T(128)}, u32[]{:S(2)}) copy-start(s32[2]{0:T(128)} %pad_add_fusion.place_ref) | copy-start | bytes 28
  32.4 3.2 %copy-start = (bf16[4,1024,1024]{2,1,0:T(8,128)(2,1)}, bf16[4,1024,1024]{2,1,0:T(8,128)(2,1)S(1)}, u32[]{:S(2)}) copy-start(bf16[4,1024,1024]{2,1,0:T(8,128)(2,1)S(1)} %shard_map.57.table_ref) | copy-start | bytes 25165828
  62.0 3.4 %copy-start.1 = (bf16[4,1024,1024]{2,1,0:T(8,128)(2,1)S(1)}, bf16[4,1024,1024]{2,1,0:T(8,128)(2,1)}, u32[]{:S(2)}) copy-start(bf16[4,1024,1024]{2,1,0:T(8,128)(2,1)} %copy-done) | copy-start | bytes 25165828
  69.3 36.9 %copy-start.3 = (f32[512,128]{1,0:T(8,128)S(1)}, f32[512,128]{1,0:T(8,128)}, u32[]{:S(2)}) copy-start(f32[512,128]{1,0:T(8,128)} %get-tuple-element.17.after_ref.refs_0_) | copy-start | bytes 786436
  73.0 33.2 %collective-permute-start.7 = (f32[512,256]{1,0:T(8,128)}, f32[512,256]{1,0:T(8,128)S(1)}, u32[]{:S(2)}, u32[]{:S(2)}) collective-permute-start(f32[512,256]{1,0:T(8,128)} %get-tuple-element.26), channel_id=1, source_target_pairs={{0,8},{8,0},{16,24},{24,16},{1,9},{9,1},{17,25},{25,17},{2,10},{10... | collective-permute-start | bytes 1572872 | tf_op jit(solution)/shard_map/ppermute | solution.py:314
  74.0 32.1 %collective-permute-start.9 = (f32[512,256]{1,0:T(8,128)}, f32[512,256]{1,0:T(8,128)S(1)}, u32[]{:S(2)}, u32[]{:S(2)}) collective-permute-start(f32[512,256]{1,0:T(8,128)} %get-tuple-element.28), channel_id=1, source_target_pairs={{0,24},{8,16},{16,8},{24,0},{1,25},{9,17},{17,9},{25,1},{2,26},{10... | collective-permute-start | bytes 1572872 | tf_op jit(solution)/shard_map/ppermute | solution.py:314
  74.4 31.7 %collective-permute-start.8 = (f32[512,256]{1,0:T(8,128)}, f32[512,256]{1,0:T(8,128)S(1)}, u32[]{:S(2)}, u32[]{:S(2)}) collective-permute-start(f32[512,256]{1,0:T(8,128)} %get-tuple-element.27), channel_id=1, source_target_pairs={{0,16},{8,24},{16,0},{24,8},{1,17},{9,25},{17,1},{25,9},{2,18},{10... | collective-permute-start | bytes 1572872 | tf_op jit(solution)/shard_map/ppermute | solution.py:314
  75.8 24.5 %collective-permute-start.5 = (f32[512,128]{1,0:T(8,128)}, f32[512,128]{1,0:T(8,128)S(1)}, u32[]{:S(2)}, u32[]{:S(2)}) collective-permute-start(f32[512,128]{1,0:T(8,128)} %get-tuple-element.23), channel_id=1, source_target_pairs={{0,6},{1,7},{2,4},{3,5},{4,2},{5,3},{6,0},{7,1},{8,14},{9,15},{10,... | collective-permute-start | bytes 786440 | tf_op jit(solution)/shard_map/ppermute | solution.py:314
  87.0 19.1 %collective-permute-start.6 = (f32[512,128]{1,0:T(8,128)}, f32[512,128]{1,0:T(8,128)S(1)}, u32[]{:S(2)}, u32[]{:S(2)}) collective-permute-start(f32[512,128]{1,0:T(8,128)} %get-tuple-element.24), channel_id=1, source_target_pairs={{0,7},{1,6},{2,5},{3,4},{4,3},{5,2},{6,1},{7,0},{8,15},{9,14},{10,... | collective-permute-start | bytes 786440 | tf_op jit(solution)/shard_map/ppermute | solution.py:314

commit v2 on v1

--- a/solution.py
+++ b/solution.py
@@ -85,13 +85,12 @@
     )
 
 
-def fill_table(waves, table_ref):
+def fill_table(waves, table_ref, length):
     half = waves.shape[1]
-    length = 2 * half
     norm = 1.0 / math.sqrt(length)
     fine = 32
     coarse = length // 4 // fine
-    special = (waves == 0) | (waves == half)
+    special = (waves == 0) | (waves == length // 2)
     coarse_c, coarse_s = cos_sin(
         (fine * lax.broadcasted_iota(jnp.int32, (coarse, half), 0) * waves) & (length - 1), length
     )
@@ -117,27 +116,35 @@
     return split_two(x)
 
 
-def second_kernel(sizes, order_ref, field_hbm, out_hbm, field_ref, table_ref, piece_ref, sems):
+def second_kernel(sizes, tile, order_ref, field_hbm, out_hbm, field_ref, table_ref, piece_ref, sems):
     planes, rows, slab, pens = sizes
+    lanes = 128
     load = pltpu.make_async_copy(field_hbm, field_ref, sems.at[pens])
     load.start()
-    half = order_ref.shape[1] // 2
-    fill_table(order_ref[:, :half], table_ref)
+    starts = [block * slab + tile * lanes for block in range(pens // 2)]
+    waves = jnp.concatenate([order_ref[:, at : at + lanes] for at in starts], 1)
+    fill_table(waves, table_ref, order_ref.shape[1])
     load.wait()
     fields = load_quarters(field_ref)
     copies = []
-    for block in range(pens // 2):
-        here = slice(block * slab, (block + 1) * slab)
-        c, s = transform_block(fields, table_ref, order_ref[:, here], block * slab, slab)
-        for part, values in enumerate((s, c)):
-            for plane in range(planes):
-                piece_ref[block, part * planes + plane] = values[plane * rows : (plane + 1) * rows]
-        for target in (block, pens - 1 - block):
-            copy = pltpu.make_async_copy(
-                piece_ref.at[block], out_hbm.at[:, target], sems.at[target]
-            )
-            copy.start()
-            copies.append(copy)
+    for pair in range(pens // 4):
+        first = 2 * pair * lanes
+        here = waves[:, first : first + 2 * lanes]
+        c, s = transform_block(fields, table_ref, here, first, 2 * lanes)
+        for side in range(2):
+            block = 2 * pair + side
+            columns = slice(side * lanes, (side + 1) * lanes)
+            for part, values in enumerate((s, c)):
+                for plane in range(planes):
+                    piece_ref[block, part * planes + plane] = values[
+                        plane * rows : (plane + 1) * rows, columns
+                    ]
+            for target in (block, pens - 1 - block):
+                copy = pltpu.make_async_copy(
+                    piece_ref.at[block], out_hbm.at[:, target], sems.at[target]
+                )
+                copy.start()
+                copies.append(copy)
     for copy in copies:
         copy.wait()
 
@@ -148,7 +155,7 @@
     load = pltpu.make_async_copy(field_hbm, field_ref, sems.at[pens])
     load.start()
     length = order_ref.shape[1]
-    fill_table(order_ref[:, : length // 2], table_ref)
+    fill_table(order_ref[:, : length // 2], table_ref, length)
     load.wait()
     fields = load_quarters(field_ref)
     pen = place_ref[0]
@@ -185,9 +192,8 @@
 
 
 def table_kernel(after_ref, out_ref):
-    half = out_ref.shape[1]
-    length = 2 * half
-    width = half // 4
+    width = out_ref.shape[2]
+    length = 8 * width
     rows = 64
     for distance in range(4):
         for at in range(0, width, rows):
@@ -199,52 +205,57 @@
             cosine, sine = cos_sin(n & (length - 1), length)
             factor = jnp.where((n & 1) == 1, 1.0 / length, -1.0 / length)
             inverse = jnp.where(n == 0, 0.0, factor / jnp.where(n == 0, 1.0, sine))
-            parts = split_two(cosine * inverse) + split_two(inverse)
-            for column in range(4):
-                row = (column + distance) % 4
-                for i, part in enumerate(parts):
-                    wrapped = i >= 2 and row < column
-                    out_ref[
-                        i,
-                        row * width + at : row * width + at + rows,
-                        column * width : (column + 1) * width,
-                    ] = -part if wrapped else part
-
-
-def circulant_kernel(pair, place_ref, recv_ref, table_ref, turn_ref, near_ref, far_ref):
-    group = place_ref[1] ^ pair
+            here = slice(at, at + rows)
+            for i, part in enumerate(split_two(cosine * inverse)):
+                out_ref[i, distance, here, :] = part
+            for i, part in enumerate(split_two(inverse)):
+                out_ref[i, 4 + distance, here, :] = part
+                if distance:
+                    out_ref[i, 7 + distance, here, :] = -part
+
+
+def circulant_kernel(place_ref, recv_ref, table_ref, turn_ref, *out_refs):
     half = recv_ref.shape[0] // 2
+    lanes = recv_ref.shape[1]
+    width = half // 4
     top, bottom = recv_ref[:half, :], recv_ref[half:, :]
     turn = turn_ref[...]
 
-    def operands(x):
-        return [dot(part, turn).astype(bf16) for part in split_two(x)]
-
-    plus, minus = operands(top + bottom), operands(top - bottom)
-    count = half // 2
-    first = pl.multiple_of((group & 1) * count, count)
-    swapped = group >= 2
-    rows = 256
-    for at in range(0, count, rows):
-        here = pl.ds(first + at, rows)
-
-        def product(which, high, low):
-            return dot(table_ref[2 * which, here, :], high) + (
-                dot(table_ref[2 * which, here, :], low) + dot(table_ref[2 * which + 1, here, :], high)
+    def operand(x):
+        return dot(jnp.concatenate(split_two(x), 1), turn).astype(bf16)
+
+    plus, minus = operand(top + bottom), operand(top - bottom)
+    for pair in range(2):
+        group = place_ref[1] ^ pair
+        swapped = group >= 2
+        for i in range(2):
+            row = 2 * (group & 1) + i
+
+            def product(x, index):
+                high, low = [
+                    jnp.concatenate([table_ref[w, index(column)] for column in range(4)], 1)
+                    for w in range(2)
+                ]
+                both = dot(high, x)
+                return both[:, :lanes] + (both[:, lanes:] + dot(low, x[:, :lanes]))
+
+            even = product(plus, lambda column: (row - column) & 3)
+            odd = product(
+                minus, lambda column: row - column + jnp.where(row >= column, 4, 11)
             )
-
-        even, odd = product(0, *plus), product(1, *minus)
-        near_ref[at : at + rows, :] = even + jnp.where(swapped, -odd, odd)
-        far_ref[at : at + rows, :] = even + jnp.where(swapped, odd, -odd)
+            here = slice(i * width, (i + 1) * width)
+            out_refs[pair][here, :] = even + jnp.where(swapped, -odd, odd)
+            out_refs[pair + 2][here, :] = even + jnp.where(swapped, odd, -odd)
 
 
 def final_kernel(sizes, place_ref, mask_ref, *refs):
     planes, rows, slab, pens = sizes
-    firsts, seconds, out_hbm = refs[:pens], refs[pens : pens + 4], refs[pens + 4]
-    first_ref, second_ref, piece_ref, sems = refs[pens + 5 :]
     lanes = 128
     tiles = slab // lanes
     step = 2 * planes * tiles
+    count = 4 * tiles
+    firsts, seconds, out_hbm = refs[:pens], refs[pens : pens + count], refs[pens + count]
+    first_ref, second_ref, piece_ref, sems = refs[pens + count + 1 :]
     loads = [
         pltpu.make_async_copy(ref, second_ref.at[k], sems.at[2 * pens + k])
         for k, ref in enumerate(seconds)
@@ -255,31 +266,26 @@
         load.start()
     pen, group = place_ref[0], place_ref[1]
     upper = pen >= pens // 2
-    low_bit, high_bit = (group & 1) == 1, group >= 2
-    special = mask_ref[...] > 0.0
-    for load in loads[:4]:
+    for load in loads[:count]:
         load.wait()
     stores = []
     for slot in range(pens):
         source = pen ^ slot
         here = pl.ds(pl.multiple_of(source * rows, rows), rows)
-        r = [second_ref[k, here, :] for k in range(4)]
-        r = [jnp.where(low_bit, r[k ^ 1], r[k]) for k in range(4)]
-        r = [jnp.where(high_bit, r[k ^ 2], r[k]) for k in range(4)]
-        loads[4 + slot].wait()
-        for plane in range(planes):
-            s, c = r[plane], r[planes + plane]
-            pieces = (
-                jnp.where(special, 0.0, jnp.where(upper, s, -s)),
-                jnp.where(special & upper, -s, -c),
-            )
-            for part in range(2):
-                for tile in range(tiles):
+        loads[count + slot].wait()
+        for tile in range(tiles):
+            special = mask_ref[:, tile * lanes : (tile + 1) * lanes] > 0.0
+            base = 4 * jnp.where(upper, tiles - 1 - tile, tile)
+            for plane in range(planes):
+                s = second_ref[base + (plane ^ group), here, :]
+                c = second_ref[base + ((planes + plane) ^ group), here, :]
+                pieces = (
+                    jnp.where(special, 0.0, jnp.where(upper, s, -s)),
+                    jnp.where(special & upper, -s, -c),
+                )
+                for part in range(2):
                     there = pl.ds((part * tiles + tile) * planes + plane, rows, stride=step)
-                    piece_ref[slot, there, :] = (
-                        first_ref[slot, there, :]
-                        + pieces[part][:, tile * lanes : (tile + 1) * lanes]
-                    )
+                    piece_ref[slot, there, :] = first_ref[slot, there, :] + pieces[part]
         size = rows * step
         store = pltpu.make_async_copy(
             piece_ref.at[slot],
@@ -328,18 +334,26 @@
     dma = pltpu.SemaphoreType.DMA
     field = pltpu.VMEM(v.shape, f32)
     table = pltpu.VMEM((2, length_y // 4, length_y), bf16)
-    v_blocks = kernel_call(
-        functools.partial(second_kernel, sizes),
-        jax.ShapeDtypeStruct((2 * planes, pens, rows, slab), f32),
-        "vh>h",
-        flops,
-        2**22,
-        60,
-        [field, table, pltpu.VMEM((pens // 2, 2 * planes, rows, slab), f32), dma((pens + 1,))],
-    )(order, v)
-    recv = lax.all_to_all(
-        v_blocks.reshape(groups * pens, rows, slab), ("grp", "pen"), 0, 0, tiled=True
-    ).reshape(length_z, slab)
+    tiles = slab // lanes
+    recv = []
+    for tile in range(tiles):
+        v_blocks = kernel_call(
+            functools.partial(second_kernel, sizes, tile),
+            jax.ShapeDtypeStruct((2 * planes, pens, rows, lanes), f32),
+            "vh>h",
+            flops // tiles,
+            2**21,
+            60,
+            [
+                field,
+                pltpu.VMEM((2, length_y // 4, length_y // tiles), bf16),
+                pltpu.VMEM((pens // 2, 2 * planes, rows, lanes), f32),
+                dma((pens + 1,)),
+            ],
+        )(order, v)
+        v_blocks = v_blocks.reshape(groups * pens, rows, lanes)
+        v_blocks = lax.all_to_all(v_blocks, ("grp", "pen"), 0, 0, tiled=True)
+        recv.append(v_blocks.reshape(length_z, lanes))
     swap = jnp.asarray(np.eye(slab)[::-1].copy(), bf16)
     size = rows * 2 * planes * slab // lanes
     firsts = kernel_call(
@@ -353,45 +367,47 @@
     )(place, order, swap, u)
     circulant = kernel_call(
         table_kernel,
-        jax.ShapeDtypeStruct((4, length_z // 2, length_z // 2), bf16),
+        jax.ShapeDtypeStruct((2, 11, length_z // 8, length_z // 8), bf16),
         "a>v",
         2**24,
-        2**23,
+        2**21,
         16,
     )(firsts[0])
     arrived = {0: firsts[0]}
     for k in reversed(range(1, pens)):
         arrived[k] = exchange(firsts[k], "pen", k)
-    turn = jnp.where(pen >= pens // 2, swap, jnp.asarray(np.eye(slab), bf16))
-    seconds = [None] * groups
-    for pair in range(2):
-        both = kernel_call(
-            functools.partial(circulant_kernel, pair),
-            [jax.ShapeDtypeStruct((group_rows, slab), f32)] * 2,
-            "svvv>vv",
-            3 * length_z * length_z * slab // 2,
-            2**23,
+    flip = np.kron(np.eye(2), np.eye(lanes)[::-1])
+    turn = jnp.where(pen >= pens // 2, jnp.asarray(flip, bf16), jnp.asarray(np.eye(2 * lanes), bf16))
+    seconds = []
+    for tile in range(tiles):
+        parts = kernel_call(
+            circulant_kernel,
+            [jax.ShapeDtypeStruct((group_rows, lanes), f32)] * groups,
+            "svvv>vvvv",
+            3 * length_z * length_z * lanes,
+            2**22,
             20,
-        )(place, recv, circulant, turn)
-        for k, values in zip((pair, pair + 2), both):
-            seconds[k] = exchange(values, "grp", k) if k else values
+        )(place, recv[tile], circulant, turn)
+        seconds.append(parts[0])
+        for k in range(1, groups):
+            seconds.append(exchange(parts[k], "grp", k))
     mine = lax.dynamic_slice_in_dim(ky_order, pen * slab, slab)
     special = ((mine == 0) | (mine == half)).astype(f32)[None, :]
     result = kernel_call(
         functools.partial(final_kernel, sizes),
         jax.ShapeDtypeStruct((pens * size, lanes), f32),
-        "sv" + "a" * (pens + groups) + ">h",
+        "sv" + "a" * (pens + groups * tiles) + ">h",
         2**23,
         2**22,
         16,
         [
             pltpu.VMEM((pens, size, lanes), f32),
-            pltpu.VMEM((groups, group_rows, slab), f32),
+            pltpu.VMEM((groups * tiles, group_rows, lanes), f32),
             pltpu.VMEM((pens, size, lanes), f32),
-            dma((2 * pens + groups,)),
+            dma((2 * pens + groups * tiles,)),
         ],
     )(place, special, *[arrived[k] for k in range(pens)], *seconds)
-    result = result.reshape(group_rows, 2, slab // lanes, planes, lanes)
+    result = result.reshape(group_rows, 2, tiles, planes, lanes)
     return jnp.transpose(result, (0, 1, 3, 2, 4)).reshape(group_rows, 2, planes, slab)
 
 

time: 110 us -> 133 us (1.21)
  the two profiles are of different devices: /device:TPU:8 before, /device:TPU:0 now
where the time goes in v2:
time: 133 us; the launch traced here: 131 us
  waiting for transfers between devices  62.6 us (47%)
  Pallas kernels  32.1 us (24%)
  starting transfers between devices  28.2 us (21%)
  local copies, waits for them, and re-layouts  5.93 us (4%)
  other arithmetic  1.44 us (1%)
    ppermute x13, waiting for transfers between devices, exchange(): return lax.ppermute(block, axis, [(i, i ^ distance) for i in range(size)])  39.7 us
    all_to_all x2, waiting for transfers between devices, fast_path(): v_blocks = lax.all_to_all(v_blocks, ('grp', 'pen'), 0, 0, tiled=True)  22.9 us
    ppermute x13, starting transfers between devices, exchange(): return lax.ppermute(block, axis, [(i, i ^ distance) for i in range(size)])  17.3 us
    all_to_all x2, starting transfers between devices, fast_path(): v_blocks = lax.all_to_all(v_blocks, ('grp', 'pen'), 0, 0, tiled=True)  10.9 us
    pallas_call x2, Pallas kernels, fast_path(): kernel_call(functools.partial(second_kernel, sizes, tile), jax.ShapeDtype...  9.22 us
    pallas_call x2, Pallas kernels, fast_path(): kernel_call(circulant_kernel, [jax.ShapeDtypeStruct((group_rows, lanes),...  9.09 us
    pallas_call x1, Pallas kernels, fast_path(): kernel_call(functools.partial(first_kernel, sizes), [jax.ShapeDtypeStruct...  8.07 us
    unnamed x26, local copies, waits for them, and re-layouts  5.93 us
  transfers between devices with their start and end apart: 15, of which 7 were waited for; matrix products, arithmetic and copies ran while one was open for 1% of the time, Pallas kernels for 19%

profile of v2, /device:TPU:0, one launch (start us, length us, event | category | flops | bytes accessed | tf_op | source)
XLA Modules:
  0.0 130.5 jit_solution(14562802949800063380)
XLA Ops:
  0.0 4.6 %shard_map.68 = f32[4,8,64,128]{3,2,1,0:T(8,128)} custom-call(s32[1,2048]{1,0:T(1,128)} %bitcast.19, f32[128,2048]{1,0:T(8,128)} %bitcast.22), custom_call_target="tpu_custom_call" | custom-call | flops 1610612736 | bytes 2097152 | tf_op jit(solution)/shard_map/pallas_call | solution.py:340
  4.6 7.3 %all-to-all-start.1 = ((f32[32,64,128]{2,1,0:T(8,128)}), f32[32,64,128]{2,1,0:T(8,128)S(1)}, u32[]{:S(2)}, u32[]{:S(2)}) async-start(f32[32,64,128]{2,1,0:T(8,128)} %bitcast.18), calls=%async_computation.1 | async-start | bytes 2097152 | tf_op jit(solution)/shard_map/all_to_all | solution.py:355
  12.0 4.6 %shard_map.65 = f32[4,8,64,128]{3,2,1,0:T(8,128)} custom-call(s32[1,2048]{1,0:T(1,128)} %bitcast.20, f32[128,2048]{1,0:T(8,128)} %bitcast.23), custom_call_target="tpu_custom_call" | custom-call | flops 1610612736 | bytes 2097152 | tf_op jit(solution)/shard_map/pallas_call | solution.py:340
  16.6 22.9 %all-to-all-done.1 = f32[32,64,128]{2,1,0:T(8,128)S(1)} async-done(((f32[32,64,128]{2,1,0:T(8,128)}), f32[32,64,128]{2,1,0:T(8,128)S(1)}, u32[]{:S(2)}, u32[]{:S(2)}) %all-to-all-start.1) | async-done | bytes 1048608 | tf_op jit(solution)/shard_map/all_to_all | solution.py:355
  39.4 0.0 copy-start.2
  39.4 3.6 %all-to-all-start = ((f32[32,64,128]{2,1,0:T(8,128)}), f32[32,64,128]{2,1,0:T(8,128)}, u32[]{:S(2)}, u32[]{:S(2)}) async-start(f32[32,64,128]{2,1,0:T(8,128)} %bitcast.17), calls=%async_computation | async-start | bytes 2097152 | tf_op jit(solution)/shard_map/all_to_all | solution.py:355
  43.0 0.7 pad_add_fusion.place_ref
  43.7 0.0 copy-start.11
  43.7 0.0 copy-start.12
  43.7 8.1 %shard_map.64 = (f32[512,128]{1,0:T(8,128)}, f32[512,128]{1,0:T(8,128)}, f32[512,128]{1,0:T(8,128)}, f32[512,128]{1,0:T(8,128)}, f32[512,128]{1,0:T(8,128)}, /*i...) custom-call(s32[2]{0:T(128)} %pad_add_fusion.place_ref, s32[1,2048]{1,0:T(1,128)} %bitcast.21, ...), custom_call_target="tpu_custom_call" | custom-call | flops 3221225472 | bytes 4194304 | tf_op jit(solution)/shard_map/pallas_call | solution.py:359
  51.8 0.0 copy-done.2
  51.8 0.0 copy-start.10
  51.8 1.6 %collective-permute-start = (f32[512,128]{1,0:T(8,128)}, f32[512,128]{1,0:T(8,128)S(1)}, u32[]{:S(2)}, u32[]{:S(2)}) collective-permute-start(f32[512,128]{1,0:T(8,128)} %get-tuple-element.22), channel_id=1, source_target_pairs={{0,1},{1,0},{2,3},{3,2},{4,5},{5,4},{6,7},{7,6},{8,9},{9,8},{10,11... | collective-permute-start | bytes 786440 | tf_op jit(solution)/shard_map/ppermute | solution.py:320
  53.4 1.5 %collective-permute-start.1 = (f32[512,128]{1,0:T(8,128)}, f32[512,128]{1,0:T(8,128)S(1)}, u32[]{:S(2)}, u32[]{:S(2)}) collective-permute-start(f32[512,128]{1,0:T(8,128)} %get-tuple-element.23), channel_id=1, source_target_pairs={{0,2},{1,3},{2,0},{3,1},{4,6},{5,7},{6,4},{7,5},{8,10},{9,11},{10,... | collective-permute-start | bytes 786440 | tf_op jit(solution)/shard_map/ppermute | solution.py:320
  55.0 0.4 collective-permute-start.2
  55.3 2.6 %collective-permute-start.3 = (f32[512,128]{1,0:T(8,128)}, f32[512,128]{1,0:T(8,128)}, u32[]{:S(2)}, u32[]{:S(2)}) collective-permute-start(f32[512,128]{1,0:T(8,128)} %get-tuple-element.25), channel_id=1, source_target_pairs={{0,4},{1,5},{2,6},{3,7},{4,0},{5,1},{6,2},{7,3},{8,12},{9,13},{10,... | collective-permute-start | bytes 786440 | tf_op jit(solution)/shard_map/ppermute | solution.py:320
  57.9 1.4 %collective-permute-start.4 = (f32[512,128]{1,0:T(8,128)}, f32[512,128]{1,0:T(8,128)}, u32[]{:S(2)}, u32[]{:S(2)}) collective-permute-start(f32[512,128]{1,0:T(8,128)} %get-tuple-element.26), channel_id=1, source_target_pairs={{0,5},{1,4},{2,7},{3,6},{4,1},{5,0},{6,3},{7,2},{8,13},{9,12},{10,... | collective-permute-start | bytes 786440 | tf_op jit(solution)/shard_map/ppermute | solution.py:320
  59.3 0.0 copy-done.11
  59.3 0.0 copy-done.12
  59.3 0.0 copy-start
  59.3 0.9 copy-done
  60.3 2.5 %shard_map.66.table_ref = bf16[2,11,256,256]{3,2,1,0:T(8,128)(2,1)S(1)} custom-call(f32[512,128]{1,0:T(8,128)S(1)} %copy-done), custom_call_target="tpu_custom_call" | custom-call | flops 16777216 | bytes 2097152 | tf_op jit(solution)/shard_map/pallas_call | solution.py:368
  62.7 0.0 copy-done.10
  62.7 0.0 copy-done.3
  62.7 4.1 %shard_map.69 = (f32[512,128]{1,0:T(8,128)S(1)}, f32[512,128]{1,0:T(8,128)}, f32[512,128]{1,0:T(8,128)}, f32[512,128]{1,0:T(8,128)}) custom-call(s32[2]{0:T(128)S(1)} %copy-done.10, f32[2048,128]{1,0:T(8,128)S(1)} %bitcast.15, bf16[2,11,256,256]{3,2,1,0:T(8,128)(2,1)S(1)} %shard_map.66.table_ref, bf16[256,256]{1,0:T(8,128)(2,1)S(1)} %broadcast_select_fusion.turn_ref), custom_call_target="tpu_custom_call" | custom-call | flops 1610612736 | bytes 4194304 | tf_op jit(solution)/shard_map/pallas_call | solution.py:383
  66.8 0.0 copy-start.6
  66.8 0.7 copy-done.6
  67.5 0.0 collective-permute-done.refs_1_
  67.5 3.5 %collective-permute-start.5 = (f32[512,128]{1,0:T(8,128)}, f32[512,128]{1,0:T(8,128)}, u32[]{:S(2)}, u32[]{:S(2)}) collective-permute-start(f32[512,128]{1,0:T(8,128)} %get-tuple-element.27), channel_id=1, source_target_pairs={{0,6},{1,7},{2,4},{3,5},{4,2},{5,3},{6,0},{7,1},{8,14},{9,15},{10,... | collective-permute-start | bytes 786440 | tf_op jit(solution)/shard_map/ppermute | solution.py:320
  71.0 5.0 %collective-permute-done.1.refs_2_ = f32[512,128]{1,0:T(8,128)S(1)} collective-permute-done((f32[512,128]{1,0:T(8,128)}, f32[512,128]{1,0:T(8,128)S(1)}, u32[]{:S(2)}, u32[]{:S(2)}) %collective-permute-start.1) | collective-permute-done | bytes 262176 | tf_op jit(solution)/shard_map/ppermute | solution.py:320
  76.0 0.0 copy-start.4
  76.0 0.7 copy-done.4
  76.7 1.8 %collective-permute-start.6 = (f32[512,128]{1,0:T(8,128)}, f32[512,128]{1,0:T(8,128)}, u32[]{:S(2)}, u32[]{:S(2)}) collective-permute-start(f32[512,128]{1,0:T(8,128)} %get-tuple-element.28), channel_id=1, source_target_pairs={{0,7},{1,6},{2,5},{3,4},{4,3},{5,2},{6,1},{7,0},{8,15},{9,14},{10,... | collective-permute-start | bytes 786440 | tf_op jit(solution)/shard_map/ppermute | solution.py:320
  78.4 3.1 %collective-permute-done.2.refs_3_ = f32[512,128]{1,0:T(8,128)} collective-permute-done((f32[512,128]{1,0:T(8,128)}, f32[512,128]{1,0:T(8,128)}, u32[]{:S(2)}, u32[]{:S(2)}) %collective-permute-start.2) | collective-permute-done | bytes 262176 | tf_op jit(solution)/shard_map/ppermute | solution.py:320
  81.6 0.0 collective-permute-start.10
  81.6 0.0 all-to-all-done
  81.6 0.0 copy-start.1
  81.6 5.0 %shard_map.67 = (f32[512,128]{1,0:T(8,128)S(1)}, f32[512,128]{1,0:T(8,128)}, f32[512,128]{1,0:T(8,128)}, f32[512,128]{1,0:T(8,128)}) custom-call(s32[2]{0:T(128)S(1)} %copy-done.10, f32[2048,128]{1,0:T(8,128)} %bitcast.7.recv_ref, bf16[2,11,256,256]{3,2,1,0:T(8,128)(2,1)S(1)} %shard_map.66.table_ref, bf16[256,256]{1,0:T(8,128)(2,1)S(1)} %broadcast_select_fusion.turn_ref), custom_call_target="tpu_custom_call" | custom-call | flops 1610612736 | bytes 4194304 | tf_op jit(solution)/shard_map/pallas_call | solution.py:383
  86.6 0.0 copy-start.8
  86.6 0.7 copy-done.8
  87.3 0.0 collective-permute-done.3.refs_4_
  87.3 1.6 %collective-permute-start.11 = (f32[512,128]{1,0:T(8,128)}, f32[512,128]{1,0:T(8,128)S(1)}, u32[]{:S(2)}, u32[]{:S(2)}) collective-permute-start(f32[512,128]{1,0:T(8,128)} %get-tuple-element.35), channel_id=1, source_target_pairs={{0,16},{8,24},{16,0},{24,8},{1,17},{9,25},{17,1},{25,9},{2,18},{10... | collective-permute-start | bytes 786440 | tf_op jit(solution)/shard_map/ppermute | solution.py:320
  88.9 15.3 %collective-permute-done.4.refs_5_ = f32[512,128]{1,0:T(8,128)} collective-permute-done((f32[512,128]{1,0:T(8,128)}, f32[512,128]{1,0:T(8,128)}, u32[]{:S(2)}, u32[]{:S(2)}) %collective-permute-start.4) | collective-permute-done | bytes 262176 | tf_op jit(solution)/shard_map/ppermute | solution.py:320
  104.2 0.1 collective-permute-start.12
  104.3 0.0 collective-permute-done.5.refs_6_
  104.3 1.5 %collective-permute-start.7 = (f32[512,128]{1,0:T(8,128)}, f32[512,128]{1,0:T(8,128)S(1)}, u32[]{:S(2)}, u32[]{:S(2)}) collective-permute-start(f32[512,128]{1,0:T(8,128)} %get-tuple-element.30), channel_id=1, source_target_pairs={{0,8},{8,0},{16,24},{24,16},{1,9},{9,1},{17,25},{25,17},{2,10},{10... | collective-permute-start | bytes 786440 | tf_op jit(solution)/shard_map/ppermute | solution.py:320
  105.8 0.0 collective-permute-done.6.refs_7_
  105.8 0.5 collective-permute-start.8
  106.4 0.0 collective-permute-done.10.refs_13_
  106.4 0.9 collective-permute-start.9
  107.3 0.8 or_convert_fusion
  108.0 0.0 collective-permute-done.11.refs_14_
  108.0 5.0 %collective-permute-done.12.refs_15_ = f32[512,128]{1,0:T(8,128)S(1)} collective-permute-done((f32[512,128]{1,0:T(8,128)}, f32[512,128]{1,0:T(8,128)S(1)}, u32[]{:S(2)}, u32[]{:S(2)}) %collective-permute-start.12) | collective-permute-done | bytes 262176 | tf_op jit(solution)/shard_map/ppermute | solution.py:320
  113.0 0.0 collective-permute-done.7.refs_9_
  113.0 5.7 %collective-permute-done.8.refs_10_ = f32[512,128]{1,0:T(8,128)S(1)} collective-permute-done((f32[512,128]{1,0:T(8,128)}, f32[512,128]{1,0:T(8,128)S(1)}, u32[]{:S(2)}, u32[]{:S(2)}) %collective-permute-start.8) | collective-permute-done | bytes 262176 | tf_op jit(solution)/shard_map/ppermute | solution.py:320
  118.7 5.6 %collective-permute-done.9.refs_11_ = f32[512,128]{1,0:T(8,128)S(1)} collective-permute-done((f32[512,128]{1,0:T(8,128)}, f32[512,128]{1,0:T(8,128)S(1)}, u32[]{:S(2)}, u32[]{:S(2)}) %collective-permute-start.9) | collective-permute-done | bytes 262176 | tf_op jit(solution)/shard_map/ppermute | solution.py:320
  124.3 0.0 copy-done.1
  124.3 0.0 copy-start.5
  124.3 0.9 copy-done.5
  125.2 0.0 copy-start.7
  125.2 0.9 copy-done.7
  126.2 0.0 copy-start.9
  126.2 0.9 copy-done.9
  127.1 3.2 %shard_map.70 = f32[4096,128]{1,0:T(8,128)} custom-call(s32[2]{0:T(128)S(1)} %copy-done.10, f32[1,256]{1,0:T(1,128)S(1)} %bitcast.16, f32[512,128]{1,0:T(8,128)S(1)} %copy-done.1, f32[512,128]{1,0:T(8,128)S(1)} %collective-permute-done.refs_1_, f32[512,128]{1,0:T(8,128)S(1)} %copy-done.5, f32[512,128]{1,0:T(8,128)} %collective-permute-done.2.refs_3_, ...), custom_call_target="tpu_custom_call" | custom-call | flops 8388608 | bytes 4194304 | tf_op jit(solution)/shard_map/pallas_call | solution.py:396
  (2 shorter events, 0.0 us)
Async XLA Ops:
  4.6 34.8 %all-to-all-start.1 = ((f32[32,64,128]{2,1,0:T(8,128)}), f32[32,64,128]{2,1,0:T(8,128)S(1)}, u32[]{:S(2)}, u32[]{:S(2)}) async-start(f32[32,64,128]{2,1,0:T(8,128)} %bitcast.18), calls=%async_computation.1 | async-start | bytes 2097152 | tf_op jit(solution)/shard_map/all_to_all | solution.py:355
  39.4 12.3 %copy-start.2 = (f32[32,64,128]{2,1,0:T(8,128)}, f32[32,64,128]{2,1,0:T(8,128)S(1)}, u32[]{:S(2)}) copy-start(f32[32,64,128]{2,1,0:T(8,128)S(1)} %all-to-all-done.1) | copy-start | bytes 3145732
  39.4 42.1 %all-to-all-start = ((f32[32,64,128]{2,1,0:T(8,128)}), f32[32,64,128]{2,1,0:T(8,128)}, u32[]{:S(2)}, u32[]{:S(2)}) async-start(f32[32,64,128]{2,1,0:T(8,128)} %bitcast.17), calls=%async_computation | async-start | bytes 2097152 | tf_op jit(solution)/shard_map/all_to_all | solution.py:355
  43.7 15.6 %copy-start.11 = (bf16[256,256]{1,0:T(8,128)(2,1)S(1)}, bf16[256,256]{1,0:T(8,128)(2,1)}, u32[]{:S(2)}) copy-start(bf16[256,256]{1,0:T(8,128)(2,1)} %constant.27.clone) | copy-start | bytes 393220
  43.7 15.6 %copy-start.12 = (bf16[256,256]{1,0:T(8,128)(2,1)S(1)}, bf16[256,256]{1,0:T(8,128)(2,1)}, u32[]{:S(2)}) copy-start(bf16[256,256]{1,0:T(8,128)(2,1)} %constant.26.clone) | copy-start | bytes 393220
  51.8 10.9 %copy-start.10 = (s32[2]{0:T(128)S(1)}, s32[2]{0:T(128)}, u32[]{:S(2)}) copy-start(s32[2]{0:T(128)} %pad_add_fusion.place_ref) | copy-start | bytes 28
  51.8 15.7 %collective-permute-start = (f32[512,128]{1,0:T(8,128)}, f32[512,128]{1,0:T(8,128)S(1)}, u32[]{:S(2)}, u32[]{:S(2)}) collective-permute-start(f32[512,128]{1,0:T(8,128)} %get-tuple-element.22), channel_id=1, source_target_pairs={{0,1},{1,0},{2,3},{3,2},{4,5},{5,4},{6,7},{7,6},{8,9},{9,8},{10,11... | collective-permute-start | bytes 786440 | tf_op jit(solution)/shard_map/ppermute | solution.py:320
  53.4 22.6 %collective-permute-start.1 = (f32[512,128]{1,0:T(8,128)}, f32[512,128]{1,0:T(8,128)S(1)}, u32[]{:S(2)}, u32[]{:S(2)}) collective-permute-start(f32[512,128]{1,0:T(8,128)} %get-tuple-element.23), channel_id=1, source_target_pairs={{0,2},{1,3},{2,0},{3,1},{4,6},{5,7},{6,4},{7,5},{8,10},{9,11},{10,... | collective-permute-start | bytes 786440 | tf_op jit(solution)/shard_map/ppermute | solution.py:320
  55.0 26.6 %collective-permute-start.2 = (f32[512,128]{1,0:T(8,128)}, f32[512,128]{1,0:T(8,128)}, u32[]{:S(2)}, u32[]{:S(2)}) collective-permute-start(f32[512,128]{1,0:T(8,128)} %get-tuple-element.24), channel_id=1, source_target_pairs={{0,3},{1,2},{2,1},{3,0},{4,7},{5,6},{6,5},{7,4},{8,11},{9,10},{10,... | collective-permute-start | bytes 786440 | tf_op jit(solution)/shard_map/ppermute | solution.py:320
  55.3 32.0 %collective-permute-start.3 = (f32[512,128]{1,0:T(8,128)}, f32[512,128]{1,0:T(8,128)}, u32[]{:S(2)}, u32[]{:S(2)}) collective-permute-start(f32[512,128]{1,0:T(8,128)} %get-tuple-element.25), channel_id=1, source_target_pairs={{0,4},{1,5},{2,6},{3,7},{4,0},{5,1},{6,2},{7,3},{8,12},{9,13},{10,... | collective-permute-start | bytes 786440 | tf_op jit(solution)/shard_map/ppermute | solution.py:320
  57.9 46.3 %collective-permute-start.4 = (f32[512,128]{1,0:T(8,128)}, f32[512,128]{1,0:T(8,128)}, u32[]{:S(2)}, u32[]{:S(2)}) collective-permute-start(f32[512,128]{1,0:T(8,128)} %get-tuple-element.26), channel_id=1, source_target_pairs={{0,5},{1,4},{2,7},{3,6},{4,1},{5,0},{6,3},{7,2},{8,13},{9,12},{10,... | collective-permute-start | bytes 786440 | tf_op jit(solution)/shard_map/ppermute | solution.py:320
  59.3 1.0 copy-start
  60.3 2.5 %copy-start.3 = (f32[32,64,128]{2,1,0:T(8,128)S(1)}, f32[32,64,128]{2,1,0:T(8,128)}, u32[]{:S(2)}) copy-start(f32[32,64,128]{2,1,0:T(8,128)} %copy-done.2) | copy-start | bytes 3145732
  66.8 0.7 copy-start.6
  67.5 36.8 %collective-permute-start.5 = (f32[512,128]{1,0:T(8,128)}, f32[512,128]{1,0:T(8,128)}, u32[]{:S(2)}, u32[]{:S(2)}) collective-permute-start(f32[512,128]{1,0:T(8,128)} %get-tuple-element.27), channel_id=1, source_target_pairs={{0,6},{1,7},{2,4},{3,5},{4,2},{5,3},{6,0},{7,1},{8,14},{9,15},{10,... | collective-permute-start | bytes 786440 | tf_op jit(solution)/shard_map/ppermute | solution.py:320
  76.0 0.7 copy-start.4
  76.7 29.2 %collective-permute-start.6 = (f32[512,128]{1,0:T(8,128)}, f32[512,128]{1,0:T(8,128)}, u32[]{:S(2)}, u32[]{:S(2)}) collective-permute-start(f32[512,128]{1,0:T(8,128)} %get-tuple-element.28), channel_id=1, source_target_pairs={{0,7},{1,6},{2,5},{3,4},{4,3},{5,2},{6,1},{7,0},{8,15},{9,14},{10,... | collective-permute-start | bytes 786440 | tf_op jit(solution)/shard_map/ppermute | solution.py:320
  81.6 24.8 %collective-permute-start.10 = (f32[512,128]{1,0:T(8,128)}, f32[512,128]{1,0:T(8,128)}, u32[]{:S(2)}, u32[]{:S(2)}) collective-permute-start(f32[512,128]{1,0:T(8,128)} %get-tuple-element.34), channel_id=1, source_target_pairs={{0,8},{8,0},{16,24},{24,16},{1,9},{9,1},{17,25},{25,17},{2,10},{10... | collective-permute-start | bytes 786440 | tf_op jit(solution)/shard_map/ppermute | solution.py:320
  81.6 42.7 %copy-start.1 = (f32[512,128]{1,0:T(8,128)S(1)}, f32[512,128]{1,0:T(8,128)}, u32[]{:S(2)}) copy-start(f32[512,128]{1,0:T(8,128)} %get-tuple-element.21.after_ref.refs_0_) | copy-start | bytes 786436
  86.6 0.7 copy-start.8
  87.3 20.7 %collective-permute-start.11 = (f32[512,128]{1,0:T(8,128)}, f32[512,128]{1,0:T(8,128)S(1)}, u32[]{:S(2)}, u32[]{:S(2)}) collective-permute-start(f32[512,128]{1,0:T(8,128)} %get-tuple-element.35), channel_id=1, source_target_pairs={{0,16},{8,24},{16,0},{24,8},{1,17},{9,25},{17,1},{25,9},{2,18},{10... | collective-permute-start | bytes 786440 | tf_op jit(solution)/shard_map/ppermute | solution.py:320
  104.2 8.8 %collective-permute-start.12 = (f32[512,128]{1,0:T(8,128)}, f32[512,128]{1,0:T(8,128)S(1)}, u32[]{:S(2)}, u32[]{:S(2)}) collective-permute-start(f32[512,128]{1,0:T(8,128)} %get-tuple-element.36), channel_id=1, source_target_pairs={{0,24},{8,16},{16,8},{24,0},{1,25},{9,17},{17,9},{25,1},{2,26},{10... | collective-permute-start | bytes 786440 | tf_op jit(solution)/shard_map/ppermute | solution.py:320
  104.3 8.7 %collective-permute-start.7 = (f32[512,128]{1,0:T(8,128)}, f32[512,128]{1,0:T(8,128)S(1)}, u32[]{:S(2)}, u32[]{:S(2)}) collective-permute-start(f32[512,128]{1,0:T(8,128)} %get-tuple-element.30), channel_id=1, source_target_pairs={{0,8},{8,0},{16,24},{24,16},{1,9},{9,1},{17,25},{25,17},{2,10},{10... | collective-permute-start | bytes 786440 | tf_op jit(solution)/shard_map/ppermute | solution.py:320
  105.8 12.9 %collective-permute-start.8 = (f32[512,128]{1,0:T(8,128)}, f32[512,128]{1,0:T(8,128)S(1)}, u32[]{:S(2)}, u32[]{:S(2)}) collective-permute-start(f32[512,128]{1,0:T(8,128)} %get-tuple-element.31), channel_id=1, source_target_pairs={{0,16},{8,24},{16,0},{24,8},{1,17},{9,25},{17,1},{25,9},{2,18},{10... | collective-permute-start | bytes 786440 | tf_op jit(solution)/shard_map/ppermute | solution.py:320
  106.4 17.9 %collective-permute-start.9 = (f32[512,128]{1,0:T(8,128)}, f32[512,128]{1,0:T(8,128)S(1)}, u32[]{:S(2)}, u32[]{:S(2)}) collective-permute-start(f32[512,128]{1,0:T(8,128)} %get-tuple-element.32), channel_id=1, source_target_pairs={{0,24},{8,16},{16,8},{24,0},{1,25},{9,17},{17,9},{25,1},{2,26},{10... | collective-permute-start | bytes 786440 | tf_op jit(solution)/shard_map/ppermute | solution.py:320
  124.3 1.0 copy-start.5
  125.2 0.9 copy-start.7
  126.2 0.9 copy-start.9

commit v3 on v2

--- a/solution.py
+++ b/solution.py
@@ -10,6 +10,8 @@
 from jax.sharding import PartitionSpec as P
 
 
+LAST = (5, 6)
+SLOTS = (0, 1, 2, 3)
 f32 = jnp.float32
 bf16 = jnp.bfloat16
 
@@ -116,11 +118,16 @@
     return split_two(x)
 
 
-def second_kernel(sizes, tile, order_ref, field_hbm, out_hbm, field_ref, table_ref, piece_ref, sems):
+def second_kernel(
+    sizes, tile, order_hbm, field_hbm, out_hbm, order_ref, field_ref, table_ref, piece_ref, sems
+):
     planes, rows, slab, pens = sizes
     lanes = 128
+    first_load = pltpu.make_async_copy(order_hbm, order_ref, sems.at[pens + 1])
+    first_load.start()
     load = pltpu.make_async_copy(field_hbm, field_ref, sems.at[pens])
     load.start()
+    first_load.wait()
     starts = [block * slab + tile * lanes for block in range(pens // 2)]
     waves = jnp.concatenate([order_ref[:, at : at + lanes] for at in starts], 1)
     fill_table(waves, table_ref, order_ref.shape[1])
@@ -141,7 +148,7 @@
                     ]
             for target in (block, pens - 1 - block):
                 copy = pltpu.make_async_copy(
-                    piece_ref.at[block], out_hbm.at[:, target], sems.at[target]
+                    piece_ref.at[block], out_hbm.at[target], sems.at[target]
                 )
                 copy.start()
                 copies.append(copy)
@@ -149,41 +156,42 @@
         copy.wait()
 
 
-def first_kernel(sizes, place_ref, order_ref, swap_ref, field_hbm, *refs):
+def first_kernel(sizes, slots, place_ref, order_ref, swap_ref, field_hbm, *refs):
     planes, rows, slab, pens = sizes
-    outs, (field_ref, table_ref, piece_ref, sems) = refs[:pens], refs[pens:]
+    outs, (field_ref, table_ref, waves_ref, piece_ref, sems) = refs[:-5], refs[-5:]
     load = pltpu.make_async_copy(field_hbm, field_ref, sems.at[pens])
     load.start()
     length = order_ref.shape[1]
-    fill_table(order_ref[:, : length // 2], table_ref, length)
+    pen = place_ref[0]
+    upper = pen >= pens // 2
+    for i, slot in enumerate(slots):
+        target = pen ^ slot
+        block = jnp.where(upper, pens - 1 - target, target)
+        first = pl.multiple_of(block * slab, slab)
+        waves_ref[:, i * slab : (i + 1) * slab] = order_ref[:, pl.ds(first, slab)]
+    fill_table(waves_ref[...], table_ref, length)
     load.wait()
     fields = load_quarters(field_ref)
-    pen = place_ref[0]
-    upper = pen >= pens // 2
     lanes = 128
     step = 2 * planes * (slab // lanes)
     copies = []
-    for slot in range(pens // 2):
-        target = pen ^ slot
-        block = jnp.where(upper, pens - 1 - target, target)
-        first = pl.multiple_of(block * slab, slab)
-        waves = order_ref[:, pl.ds(first, slab)]
-        c, s = transform_block(fields, table_ref, waves, first, slab)
+    for i in range(len(slots)):
+        waves = waves_ref[:, i * slab : (i + 1) * slab]
+        c, s = transform_block(fields, table_ref, waves, i * slab, slab)
         scale = signed_scale(waves, length)
-        opposite = slot ^ (pens - 1)
         for part, values in enumerate((scale * s, scale * c)):
             turned = reverse_lanes(values, swap_ref[...])
             if part == 1:
                 turned = -turned
             near, far = jnp.where(upper, turned, values), jnp.where(upper, values, turned)
-            for to, piece in ((slot, near), (opposite, far)):
+            for to, piece in ((2 * i, near), (2 * i + 1, far)):
                 for plane in range(planes):
                     for tile in range(slab // lanes):
                         at = (part * (slab // lanes) + tile) * planes + plane
                         piece_ref[to, pl.ds(at, rows, stride=step), :] = piece[
                             plane * rows : (plane + 1) * rows, tile * lanes : (tile + 1) * lanes
                         ]
-        for to in (slot, opposite):
+        for to in (2 * i, 2 * i + 1):
             copy = pltpu.make_async_copy(piece_ref.at[to], outs[to], sems.at[to])
             copy.start()
             copies.append(copy)
@@ -215,11 +223,15 @@
 
 
 def circulant_kernel(place_ref, recv_ref, table_ref, turn_ref, *out_refs):
-    half = recv_ref.shape[0] // 2
-    lanes = recv_ref.shape[1]
-    width = half // 4
-    top, bottom = recv_ref[:half, :], recv_ref[half:, :]
+    count, rows, lanes = recv_ref.shape
+    width = count * rows // 8
     turn = turn_ref[...]
+    top, bottom = [
+        jnp.concatenate(
+            [recv_ref[4 * pen + group] for group in groups for pen in range(count // 4)], 0
+        )
+        for groups in ((0, 1), (2, 3))
+    ]
 
     def operand(x):
         return dot(jnp.concatenate(split_two(x), 1), turn).astype(bf16)
@@ -232,12 +244,15 @@
             row = 2 * (group & 1) + i
 
             def product(x, index):
-                high, low = [
-                    jnp.concatenate([table_ref[w, index(column)] for column in range(4)], 1)
-                    for w in range(2)
-                ]
-                both = dot(high, x)
-                return both[:, :lanes] + (both[:, lanes:] + dot(low, x[:, :lanes]))
+                both = jnp.concatenate(
+                    [
+                        jnp.concatenate([table_ref[w, index(column)] for column in range(4)], 1)
+                        for w in range(2)
+                    ],
+                    0,
+                )
+                both = dot(both, x)
+                return both[:width, :lanes] + (both[:width, lanes:] + both[width:, :lanes])
 
             even = product(plus, lambda column: (row - column) & 3)
             odd = product(
@@ -248,49 +263,69 @@
             out_refs[pair + 2][here, :] = even + jnp.where(swapped, odd, -odd)
 
 
-def final_kernel(sizes, place_ref, mask_ref, *refs):
+def final_kernel(sizes, slots, place_ref, order_ref, *refs):
     planes, rows, slab, pens = sizes
     lanes = 128
     tiles = slab // lanes
     step = 2 * planes * tiles
+    size = rows * step
     count = 4 * tiles
-    firsts, seconds, out_hbm = refs[:pens], refs[pens : pens + count], refs[pens + count]
-    first_ref, second_ref, piece_ref, sems = refs[pens + count + 1 :]
-    loads = [
-        pltpu.make_async_copy(ref, second_ref.at[k], sems.at[2 * pens + k])
-        for k, ref in enumerate(seconds)
-    ] + [
-        pltpu.make_async_copy(ref, first_ref.at[k], sems.at[k]) for k, ref in enumerate(firsts)
-    ]
-    for load in loads:
-        load.start()
+    firsts, seconds = refs[: len(slots)], refs[len(slots) : len(slots) + count]
+    out_hbm, late_ref, piece_ref, sems = refs[-4:]
     pen, group = place_ref[0], place_ref[1]
     upper = pen >= pens // 2
-    for load in loads[:count]:
-        load.wait()
+    low_bit, high_bit = (group & 1) == 1, group >= 2
+    waves = order_ref[:, pl.ds(pl.multiple_of(pen * slab, slab), slab)]
+    specials = (waves == 0) | (waves == order_ref.shape[1] // 2)
     stores = []
-    for slot in range(pens):
+    others = [slot for slot in range(1, pens) if slot not in slots]
+    for at, slot in enumerate([*slots, *others]):
         source = pen ^ slot
         here = pl.ds(pl.multiple_of(source * rows, rows), rows)
-        loads[count + slot].wait()
+        early = at < len(slots)
+        r = [ref[here, :] for ref in seconds]
+        r = [jnp.where(low_bit, r[k ^ 1], r[k]) for k in range(count)]
+        r = [jnp.where(high_bit, r[k ^ 2], r[k]) for k in range(count)]
+        if tiles == 2:
+            r = [jnp.where(upper, r[k ^ 4], r[k]) for k in range(count)]
         for tile in range(tiles):
-            special = mask_ref[:, tile * lanes : (tile + 1) * lanes] > 0.0
-            base = 4 * jnp.where(upper, tiles - 1 - tile, tile)
+            special = specials[:, tile * lanes : (tile + 1) * lanes]
+            base = 4 * tile
             for plane in range(planes):
-                s = second_ref[base + (plane ^ group), here, :]
-                c = second_ref[base + ((planes + plane) ^ group), here, :]
+                s, c = r[base + plane], r[base + planes + plane]
                 pieces = (
                     jnp.where(special, 0.0, jnp.where(upper, s, -s)),
                     jnp.where(special & upper, -s, -c),
                 )
                 for part in range(2):
                     there = pl.ds((part * tiles + tile) * planes + plane, rows, stride=step)
-                    piece_ref[slot, there, :] = first_ref[slot, there, :] + pieces[part]
-        size = rows * step
+                    if early:
+                        piece_ref[at, there, :] = firsts[at][there, :] + pieces[part]
+                    else:
+                        late_ref[at - len(slots), there, :] = pieces[part]
+        if early:
+            store = pltpu.make_async_copy(
+                piece_ref.at[at],
+                out_hbm.at[pl.ds(pl.multiple_of(source * size, size), size)],
+                sems.at[at],
+            )
+            store.start()
+            stores.append(store)
+    for store in stores:
+        store.wait()
+
+
+def last_kernel(slots, place_ref, late_ref, *refs):
+    firsts, (before_hbm, out_hbm, piece_ref, sems) = refs[: len(slots)], refs[len(slots) :]
+    size = late_ref.shape[1]
+    stores = []
+    for at, slot in enumerate(slots):
+        source = place_ref[0] ^ slot
+        piece_ref[at] = firsts[at][...] + late_ref[at]
         store = pltpu.make_async_copy(
-            piece_ref.at[slot],
+            piece_ref.at[at],
             out_hbm.at[pl.ds(pl.multiple_of(source * size, size), size)],
-            sems.at[pens + slot],
+            sems.at[at],
         )
         store.start()
         stores.append(store)
@@ -301,7 +336,7 @@
 SPACES = {"s": pltpu.SMEM, "v": pltpu.VMEM, "h": pltpu.HBM, "a": pl.ANY}
 
 
-def kernel_call(body, shapes, spaces, flops, moved, limit, scratch=()):
+def kernel_call(body, shapes, spaces, flops, moved, limit, scratch=(), aliases=None):
     inputs, outputs = spaces.split(">")
     specs = [pl.BlockSpec(memory_space=SPACES[s]) for s in outputs]
     return pl.pallas_call(
@@ -310,6 +345,7 @@
         in_specs=[pl.BlockSpec(memory_space=SPACES[s]) for s in inputs],
         out_specs=specs if isinstance(shapes, list) else specs[0],
         scratch_shapes=scratch,
+        input_output_aliases=aliases or {},
         cost_estimate=pl.CostEstimate(flops=flops, bytes_accessed=moved, transcendentals=0),
         compiler_params=pltpu.CompilerParams(vmem_limit_bytes=limit * 2**20),
     )
@@ -325,7 +361,6 @@
     length_y = v.shape[1]
     group_rows = rows * pens
     length_z = group_rows * groups
-    half = length_y // 2
     lanes = 128
     pen, group = lax.axis_index("pen"), lax.axis_index("grp")
     place = jnp.stack([pen, group]).astype(jnp.int32)
@@ -333,38 +368,50 @@
     flops = 2 * 3 * planes * rows * length_y * length_y
     dma = pltpu.SemaphoreType.DMA
     field = pltpu.VMEM(v.shape, f32)
-    table = pltpu.VMEM((2, length_y // 4, length_y), bf16)
     tiles = slab // lanes
     recv = []
     for tile in range(tiles):
         v_blocks = kernel_call(
             functools.partial(second_kernel, sizes, tile),
-            jax.ShapeDtypeStruct((2 * planes, pens, rows, lanes), f32),
-            "vh>h",
+            jax.ShapeDtypeStruct((pens, 2 * planes, rows, lanes), f32),
+            "hh>h",
             flops // tiles,
             2**21,
             60,
             [
+                pltpu.VMEM((1, length_y), jnp.int32),
                 field,
                 pltpu.VMEM((2, length_y // 4, length_y // tiles), bf16),
                 pltpu.VMEM((pens // 2, 2 * planes, rows, lanes), f32),
-                dma((pens + 1,)),
+                dma((pens + 2,)),
             ],
         )(order, v)
         v_blocks = v_blocks.reshape(groups * pens, rows, lanes)
-        v_blocks = lax.all_to_all(v_blocks, ("grp", "pen"), 0, 0, tiled=True)
-        recv.append(v_blocks.reshape(length_z, lanes))
+        recv.append(lax.all_to_all(v_blocks, ("pen", "grp"), 0, 0, tiled=True))
     swap = jnp.asarray(np.eye(slab)[::-1].copy(), bf16)
     size = rows * 2 * planes * slab // lanes
-    firsts = kernel_call(
-        functools.partial(first_kernel, sizes),
-        [jax.ShapeDtypeStruct((size, lanes), f32)] * pens,
-        "svvh>" + "h" * pens,
-        flops,
-        2**22,
-        60,
-        [field, table, pltpu.VMEM((pens, size, lanes), f32), dma((pens + 1,))],
-    )(place, order, swap, u)
+    firsts = [None] * pens
+    for slots in (SLOTS, [k for k in range(pens // 2) if k not in SLOTS]):
+        if not slots:
+            continue
+        wide = len(slots) * slab
+        pieces = kernel_call(
+            functools.partial(first_kernel, sizes, slots),
+            [jax.ShapeDtypeStruct((size, lanes), f32)] * (2 * len(slots)),
+            "svvh>" + "h" * (2 * len(slots)),
+            flops // pens * len(slots),
+            2**21,
+            60,
+            [
+                field,
+                pltpu.VMEM((2, length_y // 4, 2 * wide), bf16),
+                pltpu.VMEM((1, wide), jnp.int32),
+                pltpu.VMEM((2 * len(slots), size, lanes), f32),
+                dma((pens + 1,)),
+            ],
+        )(place, order, swap, u)
+        for k, slot in enumerate(slots):
+            firsts[slot], firsts[pens - 1 - slot] = pieces[2 * k], pieces[2 * k + 1]
     circulant = kernel_call(
         table_kernel,
         jax.ShapeDtypeStruct((2, 11, length_z // 8, length_z // 8), bf16),
@@ -372,7 +419,7 @@
         2**24,
         2**21,
         16,
-    )(firsts[0])
+    )(firsts[pens // 2])
     arrived = {0: firsts[0]}
     for k in reversed(range(1, pens)):
         arrived[k] = exchange(firsts[k], "pen", k)
@@ -391,22 +438,29 @@
         seconds.append(parts[0])
         for k in range(1, groups):
             seconds.append(exchange(parts[k], "grp", k))
-    mine = lax.dynamic_slice_in_dim(ky_order, pen * slab, slab)
-    special = ((mine == 0) | (mine == half)).astype(f32)[None, :]
+    slots = [k for k in range(pens) if k not in LAST]
+    result, late = kernel_call(
+        functools.partial(final_kernel, sizes, slots),
+        [
+            jax.ShapeDtypeStruct((pens * size, lanes), f32),
+            jax.ShapeDtypeStruct((len(LAST), size, lanes), f32),
+        ],
+        "sv" + "v" * (len(slots) + groups * tiles) + ">hv",
+        2**20,
+        2**20,
+        16,
+        [pltpu.VMEM((len(slots), size, lanes), f32), dma((pens,))],
+    )(place, order, *[arrived[k] for k in slots], *seconds)
     result = kernel_call(
-        functools.partial(final_kernel, sizes),
-        jax.ShapeDtypeStruct((pens * size, lanes), f32),
-        "sv" + "a" * (pens + groups * tiles) + ">h",
-        2**23,
-        2**22,
-        16,
-        [
-            pltpu.VMEM((pens, size, lanes), f32),
-            pltpu.VMEM((groups * tiles, group_rows, lanes), f32),
-            pltpu.VMEM((pens, size, lanes), f32),
-            dma((2 * pens + groups * tiles,)),
-        ],
-    )(place, special, *[arrived[k] for k in range(pens)], *seconds)
+        functools.partial(last_kernel, sorted(LAST)),
+        jax.ShapeDtypeStruct(result.shape, f32),
+        "sv" + "v" * len(LAST) + "h>h",
+        2**18,
+        2**18,
+        8,
+        [pltpu.VMEM((len(LAST), size, lanes), f32), dma((len(LAST),))],
+        {2 + len(LAST): 0},
+    )(place, late, *[arrived[k] for k in sorted(LAST)], result)
     result = result.reshape(group_rows, 2, tiles, planes, lanes)
     return jnp.transpose(result, (0, 1, 3, 2, 4)).reshape(group_rows, 2, planes, slab)
 

time: 133 us -> 121 us (0.910)
  the two profiles are of different devices: /device:TPU:0 before, /device:TPU:17 now
where the time goes in v3:
time: 121 us
  waiting for transfers between devices  55.8 us (46%)
  Pallas kernels  31.2 us (26%)
  starting transfers between devices  30.1 us (25%)
  local copies, waits for them, and re-layouts  2.46 us (2%)
    ppermute x13, waiting for transfers between devices, exchange(): return lax.ppermute(block, axis, [(i, i ^ distance) for i in range(size)])  34.9 us
    all_to_all x2, waiting for transfers between devices, fast_path(): recv.append(lax.all_to_all(v_blocks, ('pen', 'grp'), 0, 0, tiled=True))  20.8 us
    ppermute x13, starting transfers between devices, exchange(): return lax.ppermute(block, axis, [(i, i ^ distance) for i in range(size)])  18.8 us
    all_to_all x2, starting transfers between devices, fast_path(): recv.append(lax.all_to_all(v_blocks, ('pen', 'grp'), 0, 0, tiled=True))  11.3 us
    pallas_call x1, Pallas kernels, fast_path(): kernel_call(functools.partial(first_kernel, sizes, slots), [jax.ShapeDtyp...  8.3 us
    pallas_call x2, Pallas kernels, fast_path(): kernel_call(functools.partial(second_kernel, sizes, tile), jax.ShapeDtype...  8.22 us
    pallas_call x2, Pallas kernels, fast_path(): kernel_call(circulant_kernel, [jax.ShapeDtypeStruct((group_rows, lanes),...  8.01 us
    pallas_call x1, Pallas kernels, fast_path(): kernel_call(functools.partial(final_kernel, sizes, slots), [jax.ShapeDtyp...  2.86 us
  transfers between devices with their start and end apart: 15, of which 7 were waited for; matrix products, arithmetic and copies ran while one was open for 1% of the time, Pallas kernels for 21%

profile of v3, /device:TPU:17, one launch (start us, length us, event | category | flops | bytes accessed | tf_op | source)
XLA Modules:
  0.0 120.6 jit_solution(12636041884157552825)
XLA Ops:
  0.0 4.1 %shard_map.68 = f32[8,4,64,128]{3,2,1,0:T(8,128)} custom-call(s32[1,2048]{1,0:T(1,128)} %bitcast.12, f32[128,2048]{1,0:T(8,128)} %bitcast.18), custom_call_target="tpu_custom_call" | custom-call | flops 1610612736 | bytes 2097152 | tf_op jit(solution)/shard_map/pallas_call | solution.py:374
  4.1 6.2 %all-to-all-start.1 = ((f32[32,64,128]{2,1,0:T(8,128)}), f32[32,64,128]{2,1,0:T(8,128)S(1)}, u32[]{:S(2)}, u32[]{:S(2)}) async-start(f32[32,64,128]{2,1,0:T(8,128)} %bitcast.17), calls=%async_computation.1 | async-start | bytes 2097152 | tf_op jit(solution)/shard_map/all_to_all | solution.py:390
  10.3 4.1 %shard_map.65 = f32[8,4,64,128]{3,2,1,0:T(8,128)} custom-call(s32[1,2048]{1,0:T(1,128)} %bitcast.13, f32[128,2048]{1,0:T(8,128)} %bitcast.19), custom_call_target="tpu_custom_call" | custom-call | flops 1610612736 | bytes 2097152 | tf_op jit(solution)/shard_map/pallas_call | solution.py:374
  14.5 20.8 %all-to-all-done.1.recv_ref = f32[32,64,128]{2,1,0:T(8,128)S(1)} async-done(((f32[32,64,128]{2,1,0:T(8,128)}), f32[32,64,128]{2,1,0:T(8,128)S(1)}, u32[]{:S(2)}, u32[]{:S(2)}) %all-to-all-start.1) | async-done | bytes 1048608 | tf_op jit(solution)/shard_map/all_to_all | solution.py:390
  35.3 0.0 copy-start
  35.3 5.1 %all-to-all-start = ((f32[32,64,128]{2,1,0:T(8,128)}), f32[32,64,128]{2,1,0:T(8,128)}, u32[]{:S(2)}, u32[]{:S(2)}) async-start(f32[32,64,128]{2,1,0:T(8,128)} %bitcast.16), calls=%async_computation | async-start | bytes 2097152 | tf_op jit(solution)/shard_map/all_to_all | solution.py:390
  40.4 0.7 pad_add_fusion.place_ref
  41.1 0.0 copy-start.10
  41.1 0.0 copy-start.11
  41.1 8.3 %shard_map.64 = (f32[512,128]{1,0:T(8,128)}, f32[512,128]{1,0:T(8,128)}, f32[512,128]{1,0:T(8,128)}, f32[512,128]{1,0:T(8,128)}, f32[512,128]{1,0:T(8,128)}, /*i...) custom-call(s32[2]{0:T(128)} %pad_add_fusion.place_ref, s32[1,2048]{1,0:T(1,128)} %bitcast.14, ...), custom_call_target="tpu_custom_call" | custom-call | flops 1610612736 | bytes 2097152 | tf_op jit(solution)/shard_map/pallas_call | solution.py:398
  49.4 0.0 copy-done
  49.4 0.0 copy-start.9
  49.4 1.3 %collective-permute-start = (f32[512,128]{1,0:T(8,128)}, f32[512,128]{1,0:T(8,128)S(1)}, u32[]{:S(2)}, u32[]{:S(2)}) collective-permute-start(f32[512,128]{1,0:T(8,128)} %get-tuple-element.24), channel_id=1, source_target_pairs={{0,1},{1,0},{2,3},{3,2},{4,5},{5,4},{6,7},{7,6},{8,9},{9,8},{10,11... | collective-permute-start | bytes 786440 | tf_op jit(solution)/shard_map/ppermute | solution.py:356
  50.7 1.2 %collective-permute-start.1 = (f32[512,128]{1,0:T(8,128)}, f32[512,128]{1,0:T(8,128)S(1)}, u32[]{:S(2)}, u32[]{:S(2)}) collective-permute-start(f32[512,128]{1,0:T(8,128)} %get-tuple-element.25), channel_id=1, source_target_pairs={{0,2},{1,3},{2,0},{3,1},{4,6},{5,7},{6,4},{7,5},{8,10},{9,11},{10,... | collective-permute-start | bytes 786440 | tf_op jit(solution)/shard_map/ppermute | solution.py:356
  51.9 0.2 collective-permute-start.2
  52.1 1.2 collective-permute-start.4
  53.3 3.1 %collective-permute-start.3 = (f32[512,128]{1,0:T(8,128)}, f32[512,128]{1,0:T(8,128)}, u32[]{:S(2)}, u32[]{:S(2)}) collective-permute-start(f32[512,128]{1,0:T(8,128)} %get-tuple-element.27.after_ref), channel_id=1, source_target_pairs={{0,4},{1,5},{2,6},{3,7},{4,0},{5,1},{6,2},{7,3},{8,12},{9,13},{10,... | collective-permute-start | bytes 786440 | tf_op jit(solution)/shard_map/ppermute | solution.py:356
  56.4 0.0 copy-done.10
  56.4 0.0 copy-done.11
  56.4 0.0 copy-start.1
  56.4 0.0 copy-start.2
  56.4 1.0 copy-done.2
  57.4 2.5 %shard_map.66.table_ref = bf16[2,11,256,256]{3,2,1,0:T(8,128)(2,1)S(1)} custom-call(f32[512,128]{1,0:T(8,128)S(1)} %copy-done.2), custom_call_target="tpu_custom_call" | custom-call | flops 16777216 | bytes 2097152 | tf_op jit(solution)/shard_map/pallas_call | solution.py:415
  59.9 0.0 copy-done.9
  59.9 0.0 copy-done.1
  59.9 4.0 %shard_map.69 = (f32[512,128]{1,0:T(8,128)S(1)}, f32[512,128]{1,0:T(8,128)}, f32[512,128]{1,0:T(8,128)}, f32[512,128]{1,0:T(8,128)}) custom-call(s32[2]{0:T(128)S(1)} %copy-done.9, f32[32,64,128]{2,1,0:T(8,128)S(1)} %copy-done.1, bf16[2,11,256,256]{3,2,1,0:T(8,128)(2,1)S(1)} %shard_map.66.table_ref, bf16[256,256]{1,0:T(8,128)(2,1)S(1)} %broadcast_select_fusion.turn_ref), custom_call_target="tpu_custom_call" | custom-call | flops 1610612736 | bytes 4194304 | tf_op jit(solution)/shard_map/pallas_call | solution.py:430
  64.0 0.0 copy-start.6
  64.0 0.7 copy-done.6
  64.7 0.0 collective-permute-done.refs_1_
  64.7 1.8 %collective-permute-start.8 = (f32[512,128]{1,0:T(8,128)}, f32[512,128]{1,0:T(8,128)}, u32[]{:S(2)}, u32[]{:S(2)}) collective-permute-start(f32[512,128]{1,0:T(8,128)} %get-tuple-element.34), channel_id=1, source_target_pairs={{0,8},{8,0},{16,24},{24,16},{1,9},{9,1},{17,25},{25,17},{2,10},{10... | collective-permute-start | bytes 786440 | tf_op jit(solution)/shard_map/ppermute | solution.py:356
  66.4 0.0 collective-permute-done.1.refs_2_
  66.5 0.0 copy-start.4
  66.5 0.7 copy-done.4
  67.2 1.2 collective-permute-start.9
  68.4 7.4 %collective-permute-done.2.refs_3_ = f32[512,128]{1,0:T(8,128)} collective-permute-done((f32[512,128]{1,0:T(8,128)}, f32[512,128]{1,0:T(8,128)}, u32[]{:S(2)}, u32[]{:S(2)}) %collective-permute-start.2) | collective-permute-done | bytes 262176 | tf_op jit(solution)/shard_map/ppermute | solution.py:356
  75.8 0.0 copy-start.3
  75.8 0.0 copy-start.8
  75.8 2.3 %collective-permute-start.10 = (f32[512,128]{1,0:T(8,128)}, f32[512,128]{1,0:T(8,128)}, u32[]{:S(2)}, u32[]{:S(2)}) collective-permute-start(f32[512,128]{1,0:T(8,128)} %get-tuple-element.36), channel_id=1, source_target_pairs={{0,24},{8,16},{16,8},{24,0},{1,25},{9,17},{17,9},{25,1},{2,26},{10... | collective-permute-start | bytes 786440 | tf_op jit(solution)/shard_map/ppermute | solution.py:356
  78.0 0.0 all-to-all-done.recv_ref
  78.0 0.0 copy-start.7
  78.0 4.0 %shard_map.67 = (f32[512,128]{1,0:T(8,128)S(1)}, f32[512,128]{1,0:T(8,128)S(1)}, f32[512,128]{1,0:T(8,128)S(1)}, f32[512,128]{1,0:T(8,128)S(1)}) custom-call(s32[2]{0:T(128)S(1)} %copy-done.9, f32[32,64,128]{2,1,0:T(8,128)} %all-to-all-done.recv_ref, bf16[2,11,256,256]{3,2,1,0:T(8,128)(2,1)S(1)} %shard_map.66.table_ref, ...), custom_call_target="tpu_custom_call" | custom-call | flops 1610612736 | bytes 4194304 | tf_op jit(solution)/shard_map/pallas_call | solution.py:430
  82.0 0.0 collective-permute-done.4.refs_5_
  82.0 0.1 collective-permute-start.5
  82.1 7.5 %collective-permute-done.3.refs_4_ = f32[512,128]{1,0:T(8,128)} collective-permute-done((f32[512,128]{1,0:T(8,128)}, f32[512,128]{1,0:T(8,128)}, u32[]{:S(2)}, u32[]{:S(2)}) %collective-permute-start.3) | collective-permute-done | bytes 262176 | tf_op jit(solution)/shard_map/ppermute | solution.py:356
  89.6 0.8 collective-permute-start.6
  90.3 0.0 collective-permute-done.8.refs_11_
  90.3 1.9 %collective-permute-start.7 = (f32[512,128]{1,0:T(8,128)S(1)}, f32[512,128]{1,0:T(8,128)S(1)}, u32[]{:S(2)}, u32[]{:S(2)}) collective-permute-start(f32[512,128]{1,0:T(8,128)S(1)} %get-tuple-element.32), channel_id=1, source_target_pairs={{0,24},{8,16},{16,8},{24,0},{1,25},{9,17},{17,9},{25,1},{2,26},{10... | collective-permute-start | bytes 786440 | tf_op jit(solution)/shard_map/ppermute | solution.py:356
  92.2 0.0 collective-permute-done.9.refs_12_
  92.2 0.0 copy-done.13
  92.2 3.9 %collective-permute-start.11 = (f32[512,128]{1,0:T(8,128)S(1)}, f32[512,128]{1,0:T(8,128)S(1)}, u32[]{:S(2)}, u32[]{:S(2)}) collective-permute-start(f32[512,128]{1,0:T(8,128)S(1)} %copy-done.13), channel_id=1, source_target_pairs={{0,5},{1,4},{2,7},{3,6},{4,1},{5,0},{6,3},{7,2},{8,13},{9,12},{10,... | collective-permute-start | bytes 786440 | tf_op jit(solution)/shard_map/ppermute | solution.py:356
  96.1 0.0 collective-permute-done.10.refs_13_
  96.1 0.0 copy-done.12
  96.1 0.0 collective-permute-start.12
  96.1 0.0 collective-permute-done.5.refs_7_
  96.1 0.4 collective-permute-done.6.refs_8_
  96.5 6.8 %collective-permute-done.7.refs_9_ = f32[512,128]{1,0:T(8,128)S(1)} collective-permute-done((f32[512,128]{1,0:T(8,128)S(1)}, f32[512,128]{1,0:T(8,128)S(1)}, u32[]{:S(2)}, u32[]{:S(2)}) %collective-permute-start.7) | collective-permute-done | bytes 262176 | tf_op jit(solution)/shard_map/ppermute | solution.py:356
  103.2 0.0 copy-done.3
  103.2 0.0 copy-done.8
  103.2 0.0 copy-done.5
  103.2 0.0 copy-done.7
  103.2 2.9 %shard_map.70 = (f32[4096,128]{1,0:T(8,128)}, f32[2,512,128]{2,1,0:T(8,128)S(1)}) custom-call(s32[2]{0:T(128)S(1)} %copy-done.9, s32[1,2048]{1,0:T(1,128)S(1)} %bitcast.15, f32[512,128]{1,0:T(8,128)S(1)} %copy-done.3, f32[512,128]{1,0:T(8,128)S(1)} %collective-permute-done.refs_1_, f32[512,128]{1,0:T(8,128)S(1)} %copy-done.5, ...), custom_call_target="tpu_custom_call" | custom-call | flops 1048576 | bytes 1048576 | tf_op jit(solution)/shard_map/pallas_call | solution.py:442
  106.1 4.7 %collective-permute-done.11.refs_0_ = f32[512,128]{1,0:T(8,128)S(1)} collective-permute-done((f32[512,128]{1,0:T(8,128)S(1)}, f32[512,128]{1,0:T(8,128)S(1)}, u32[]{:S(2)}, u32[]{:S(2)}) %collective-permute-start.11) | collective-permute-done | bytes 262176 | tf_op jit(solution)/shard_map/ppermute | solution.py:356
  110.8 8.2 %collective-permute-done.12.refs_1_ = f32[512,128]{1,0:T(8,128)S(1)} collective-permute-done((f32[512,128]{1,0:T(8,128)S(1)}, f32[512,128]{1,0:T(8,128)S(1)}, u32[]{:S(2)}, u32[]{:S(2)}) %collective-permute-start.12) | collective-permute-done | bytes 262176 | tf_op jit(solution)/shard_map/ppermute | solution.py:356
  119.0 1.4 %shard_map.71 = f32[4096,128]{1,0:T(8,128)} custom-call(s32[2]{0:T(128)S(1)} %copy-done.9, f32[2,512,128]{2,1,0:T(8,128)S(1)} %get-tuple-element.37.late_ref, f32[512,128]{1,0:T(8,128)S(1)} %collective-permute-done.11.refs_0_, f32[512,128]{1,0:T(8,128)S(1)} %collective-permute-done.12.refs_1_, ...), custom_call_target="tpu_custom_call", output_to_operand_aliasing={{}: (4, {})} | custom-call | flops 262144 | bytes 262144 | tf_op jit(solution)/shard_map/pallas_call | solution.py:454
  (4 shorter events, 0.0 us)
Async XLA Ops:
  4.1 31.2 %all-to-all-start.1 = ((f32[32,64,128]{2,1,0:T(8,128)}), f32[32,64,128]{2,1,0:T(8,128)S(1)}, u32[]{:S(2)}, u32[]{:S(2)}) async-start(f32[32,64,128]{2,1,0:T(8,128)} %bitcast.17), calls=%async_computation.1 | async-start | bytes 2097152 | tf_op jit(solution)/shard_map/all_to_all | solution.py:390
  35.3 14.1 %copy-start = (f32[32,64,128]{2,1,0:T(8,128)}, f32[32,64,128]{2,1,0:T(8,128)S(1)}, u32[]{:S(2)}) copy-start(f32[32,64,128]{2,1,0:T(8,128)S(1)} %all-to-all-done.1.recv_ref) | copy-start | bytes 3145732
  35.3 42.7 %all-to-all-start = ((f32[32,64,128]{2,1,0:T(8,128)}), f32[32,64,128]{2,1,0:T(8,128)}, u32[]{:S(2)}, u32[]{:S(2)}) async-start(f32[32,64,128]{2,1,0:T(8,128)} %bitcast.16), calls=%async_computation | async-start | bytes 2097152 | tf_op jit(solution)/shard_map/all_to_all | solution.py:390
  41.1 15.3 %copy-start.10 = (bf16[256,256]{1,0:T(8,128)(2,1)S(1)}, bf16[256,256]{1,0:T(8,128)(2,1)}, u32[]{:S(2)}) copy-start(bf16[256,256]{1,0:T(8,128)(2,1)} %constant.18.clone) | copy-start | bytes 393220
  41.1 15.3 %copy-start.11 = (bf16[256,256]{1,0:T(8,128)(2,1)S(1)}, bf16[256,256]{1,0:T(8,128)(2,1)}, u32[]{:S(2)}) copy-start(bf16[256,256]{1,0:T(8,128)(2,1)} %constant.17.clone) | copy-start | bytes 393220
  49.4 10.5 %copy-start.9 = (s32[2]{0:T(128)S(1)}, s32[2]{0:T(128)}, u32[]{:S(2)}) copy-start(s32[2]{0:T(128)} %pad_add_fusion.place_ref) | copy-start | bytes 28
  49.4 15.2 %collective-permute-start = (f32[512,128]{1,0:T(8,128)}, f32[512,128]{1,0:T(8,128)S(1)}, u32[]{:S(2)}, u32[]{:S(2)}) collective-permute-start(f32[512,128]{1,0:T(8,128)} %get-tuple-element.24), channel_id=1, source_target_pairs={{0,1},{1,0},{2,3},{3,2},{4,5},{5,4},{6,7},{7,6},{8,9},{9,8},{10,11... | collective-permute-start | bytes 786440 | tf_op jit(solution)/shard_map/ppermute | solution.py:356
  50.7 15.8 %collective-permute-start.1 = (f32[512,128]{1,0:T(8,128)}, f32[512,128]{1,0:T(8,128)S(1)}, u32[]{:S(2)}, u32[]{:S(2)}) collective-permute-start(f32[512,128]{1,0:T(8,128)} %get-tuple-element.25), channel_id=1, source_target_pairs={{0,2},{1,3},{2,0},{3,1},{4,6},{5,7},{6,4},{7,5},{8,10},{9,11},{10,... | collective-permute-start | bytes 786440 | tf_op jit(solution)/shard_map/ppermute | solution.py:356
  51.9 23.8 %collective-permute-start.2 = (f32[512,128]{1,0:T(8,128)}, f32[512,128]{1,0:T(8,128)}, u32[]{:S(2)}, u32[]{:S(2)}) collective-permute-start(f32[512,128]{1,0:T(8,128)} %get-tuple-element.26), channel_id=1, source_target_pairs={{0,3},{1,2},{2,1},{3,0},{4,7},{5,6},{6,5},{7,4},{8,11},{9,10},{10,... | collective-permute-start | bytes 786440 | tf_op jit(solution)/shard_map/ppermute | solution.py:356
  52.1 29.9 %collective-permute-start.4 = (f32[512,128]{1,0:T(8,128)}, f32[512,128]{1,0:T(8,128)}, u32[]{:S(2)}, u32[]{:S(2)}) collective-permute-start(f32[512,128]{1,0:T(8,128)} %get-tuple-element.28), channel_id=1, source_target_pairs={{0,7},{1,6},{2,5},{3,4},{4,3},{5,2},{6,1},{7,0},{8,15},{9,14},{10,... | collective-permute-start | bytes 786440 | tf_op jit(solution)/shard_map/ppermute | solution.py:356
  53.3 36.3 %collective-permute-start.3 = (f32[512,128]{1,0:T(8,128)}, f32[512,128]{1,0:T(8,128)}, u32[]{:S(2)}, u32[]{:S(2)}) collective-permute-start(f32[512,128]{1,0:T(8,128)} %get-tuple-element.27.after_ref), channel_id=1, source_target_pairs={{0,4},{1,5},{2,6},{3,7},{4,0},{5,1},{6,2},{7,3},{8,12},{9,13},{10,... | collective-permute-start | bytes 786440 | tf_op jit(solution)/shard_map/ppermute | solution.py:356
  56.4 3.5 %copy-start.1 = (f32[32,64,128]{2,1,0:T(8,128)S(1)}, f32[32,64,128]{2,1,0:T(8,128)}, u32[]{:S(2)}) copy-start(f32[32,64,128]{2,1,0:T(8,128)} %copy-done) | copy-start | bytes 3145732
  56.4 1.0 copy-start.2
  64.0 0.7 copy-start.6
  64.7 25.7 %collective-permute-start.8 = (f32[512,128]{1,0:T(8,128)}, f32[512,128]{1,0:T(8,128)}, u32[]{:S(2)}, u32[]{:S(2)}) collective-permute-start(f32[512,128]{1,0:T(8,128)} %get-tuple-element.34), channel_id=1, source_target_pairs={{0,8},{8,0},{16,24},{24,16},{1,9},{9,1},{17,25},{25,17},{2,10},{10... | collective-permute-start | bytes 786440 | tf_op jit(solution)/shard_map/ppermute | solution.py:356
  66.5 0.7 copy-start.4
  67.2 25.0 %collective-permute-start.9 = (f32[512,128]{1,0:T(8,128)}, f32[512,128]{1,0:T(8,128)}, u32[]{:S(2)}, u32[]{:S(2)}) collective-permute-start(f32[512,128]{1,0:T(8,128)} %get-tuple-element.35), channel_id=1, source_target_pairs={{0,16},{8,24},{16,0},{24,8},{1,17},{9,25},{17,1},{25,9},{2,18},{10... | collective-permute-start | bytes 786440 | tf_op jit(solution)/shard_map/ppermute | solution.py:356
  75.8 27.4 %copy-start.3 = (f32[512,128]{1,0:T(8,128)S(1)}, f32[512,128]{1,0:T(8,128)}, u32[]{:S(2)}) copy-start(f32[512,128]{1,0:T(8,128)} %get-tuple-element.23.refs_0_) | copy-start | bytes 786436
  75.8 27.4 %copy-start.8 = (s32[2048]{0:T(1024)S(1)}, s32[2048]{0:T(1024)}, u32[]{:S(2)}) copy-start(s32[2048]{0:T(1024)} %param.8) | copy-start | bytes 24580
  75.8 20.3 %collective-permute-start.10 = (f32[512,128]{1,0:T(8,128)}, f32[512,128]{1,0:T(8,128)}, u32[]{:S(2)}, u32[]{:S(2)}) collective-permute-start(f32[512,128]{1,0:T(8,128)} %get-tuple-element.36), channel_id=1, source_target_pairs={{0,24},{8,16},{16,8},{24,0},{1,25},{9,17},{17,9},{25,1},{2,26},{10... | collective-permute-start | bytes 786440 | tf_op jit(solution)/shard_map/ppermute | solution.py:356
  78.0 14.1 %copy-start.13 = (f32[512,128]{1,0:T(8,128)S(1)}, f32[512,128]{1,0:T(8,128)}, u32[]{:S(2)}) copy-start(f32[512,128]{1,0:T(8,128)} %get-tuple-element.38) | copy-start | bytes 786436
  78.0 18.0 %copy-start.12 = (f32[512,128]{1,0:T(8,128)S(1)}, f32[512,128]{1,0:T(8,128)}, u32[]{:S(2)}) copy-start(f32[512,128]{1,0:T(8,128)} %get-tuple-element.39) | copy-start | bytes 786436
  78.0 25.2 %copy-start.5 = (f32[512,128]{1,0:T(8,128)S(1)}, f32[512,128]{1,0:T(8,128)}, u32[]{:S(2)}) copy-start(f32[512,128]{1,0:T(8,128)} %copy-done.4) | copy-start | bytes 786436
  78.0 25.2 %copy-start.7 = (f32[512,128]{1,0:T(8,128)S(1)}, f32[512,128]{1,0:T(8,128)}, u32[]{:S(2)}) copy-start(f32[512,128]{1,0:T(8,128)} %copy-done.6) | copy-start | bytes 786436
  82.0 14.1 %collective-permute-start.5 = (f32[512,128]{1,0:T(8,128)S(1)}, f32[512,128]{1,0:T(8,128)S(1)}, u32[]{:S(2)}, u32[]{:S(2)}) collective-permute-start(f32[512,128]{1,0:T(8,128)S(1)} %get-tuple-element.30), channel_id=1, source_target_pairs={{0,8},{8,0},{16,24},{24,16},{1,9},{9,1},{17,25},{25,17},{2,10},{10... | collective-permute-start | bytes 786440 | tf_op jit(solution)/shard_map/ppermute | solution.py:356
  89.6 6.9 %collective-permute-start.6 = (f32[512,128]{1,0:T(8,128)S(1)}, f32[512,128]{1,0:T(8,128)S(1)}, u32[]{:S(2)}, u32[]{:S(2)}) collective-permute-start(f32[512,128]{1,0:T(8,128)S(1)} %get-tuple-element.31), channel_id=1, source_target_pairs={{0,16},{8,24},{16,0},{24,8},{1,17},{9,25},{17,1},{25,9},{2,18},{10... | collective-permute-start | bytes 786440 | tf_op jit(solution)/shard_map/ppermute | solution.py:356
  90.3 12.9 %collective-permute-start.7 = (f32[512,128]{1,0:T(8,128)S(1)}, f32[512,128]{1,0:T(8,128)S(1)}, u32[]{:S(2)}, u32[]{:S(2)}) collective-permute-start(f32[512,128]{1,0:T(8,128)S(1)} %get-tuple-element.32), channel_id=1, source_target_pairs={{0,24},{8,16},{16,8},{24,0},{1,25},{9,17},{17,9},{25,1},{2,26},{10... | collective-permute-start | bytes 786440 | tf_op jit(solution)/shard_map/ppermute | solution.py:356
  92.2 18.6 %collective-permute-start.11 = (f32[512,128]{1,0:T(8,128)S(1)}, f32[512,128]{1,0:T(8,128)S(1)}, u32[]{:S(2)}, u32[]{:S(2)}) collective-permute-start(f32[512,128]{1,0:T(8,128)S(1)} %copy-done.13), channel_id=1, source_target_pairs={{0,5},{1,4},{2,7},{3,6},{4,1},{5,0},{6,3},{7,2},{8,13},{9,12},{10,... | collective-permute-start | bytes 786440 | tf_op jit(solution)/shard_map/ppermute | solution.py:356
  96.1 22.9 %collective-permute-start.12 = (f32[512,128]{1,0:T(8,128)S(1)}, f32[512,128]{1,0:T(8,128)S(1)}, u32[]{:S(2)}, u32[]{:S(2)}) collective-permute-start(f32[512,128]{1,0:T(8,128)S(1)} %copy-done.12), channel_id=1, source_target_pairs={{0,6},{1,7},{2,4},{3,5},{4,2},{5,3},{6,0},{7,1},{8,14},{9,15},{10,... | collective-permute-start | bytes 786440 | tf_op jit(solution)/shard_map/ppermute | solution.py:356
